TPU v7x, 256 devices: a whole 4x4x8 slice. The times are simulated.
256 devices in a mesh: az: 16 (over z, x_hi), rad: 16 (over y, x_lo, core).
Axes of the slice: x: 4 (x_hi: 2, x_lo: 2; x = x_hi * 2 + x_lo), y: 4, z: 8, core: 2. Of those that a mesh axis runs over, the one named last changes fastest.
Arguments:
- fields: float32 [8, 256, 512, 128], P(None, 'rad', 'az'), as said below
- offsets: int32 [256], replicated, may hold values from 0 to 511
- boundary_shift: int32 [1], replicated, may hold values from 0 to 511
Outputs:
- advanced: float32 [8, 256, 512, 128], P(None, 'rad', 'az')
Inputs may be any that keep to these rules, and one draw needn't show every extreme that they name: Each cell of fields is a conserved state whose density and implied pressure lie between 0.5 and 2; velocities stay under 1.8 and field components under 0.9 in magnitude.
All inputs are finite; a program needn't handle non-finite values.
Results may differ from a plain program's by a relative error of at most 0.0003.
Values sent between devices are 32-bit elements; how exact they have to be, the bound alone decides.
No kernel may reach another device: no remote copies, remote signals or barrier semaphores. Data moves between devices by JAX's collectives and lax.ppermute only.
A program may use at most 192 MiB of HBM per device.

v0:
```python
import jax
import jax.numpy as jnp
from jax import lax
from jax.sharding import Mesh
from jax.sharding import PartitionSpec as P

AZ = ("az_0", "az_1")
RAD = ("rad_0", "rad_1", "rad_2")
AZ_RAD = ("az_0", "az_1", "rad_0", "rad_1", "rad_2")


GAMMA_RATIO = 5.0 / 3.0
CFL_NUMBER = 0.4
OMEGA_RATE = 1.0
SHEAR_RATE = 1.5


def passed_along(array, axis, by):
    devices = lax.axis_size(axis)
    return lax.ppermute(array, axis, [(i, (i + by) % devices) for i in range(devices)])


def padded(block, sides, width):
    for axis, dim in sides:
        count = lax.axis_size(axis)
        forward = [(i, i + 1) for i in range(count - 1)]
        forward.append((count - 1, 0))
        backward = [(target, source) for source, target in forward]
        low = lax.ppermute(
            lax.slice_in_dim(block, block.shape[dim] - width, None, axis=dim), axis, forward
        )
        high = lax.ppermute(lax.slice_in_dim(block, 0, width, axis=dim), axis, backward)
        block = jnp.concatenate([low, block, high], axis=dim)
    return block


def one_axis_at_a_time(array, axes):
    for axis in axes:
        array = lax.pmax(array, axis)
    return array


def primitive(state):
    density = state[0]
    inverse = 1.0 / density
    speed_x = state[1] * inverse
    speed_y = state[2] * inverse
    speed_z = state[3] * inverse
    kinetic = 0.5 * density * (speed_x * speed_x + speed_y * speed_y + speed_z * speed_z)
    magnetic = 0.5 * (state[5] * state[5] + state[6] * state[6] + state[7] * state[7])
    pressure = (GAMMA_RATIO - 1.0) * (state[4] - kinetic - magnetic)
    return (density, speed_x, speed_y, speed_z, pressure, state[5], state[6], state[7])


def fast_speed(density, pressure, normal_field, field_sq):
    sound = (GAMMA_RATIO * pressure + field_sq) / density
    spread = jnp.maximum(
        sound * sound
        - 4.0 * GAMMA_RATIO * pressure * normal_field * normal_field / (density * density),
        0.0,
    )
    return jnp.sqrt(0.5 * (sound + jnp.sqrt(spread)))


def cell_speed(primitives):
    field_sq = (
        primitives[5] * primitives[5]
        + primitives[6] * primitives[6]
        + primitives[7] * primitives[7]
    )
    total = jnp.abs(primitives[1]) + fast_speed(
        primitives[0], primitives[4], primitives[5], field_sq
    )
    total = (
        total
        + jnp.abs(primitives[2])
        + fast_speed(primitives[0], primitives[4], primitives[6], field_sq)
    )
    total = (
        total
        + jnp.abs(primitives[3])
        + fast_speed(primitives[0], primitives[4], primitives[7], field_sq)
    )
    return total


def minmod(first_diff, second_diff):
    return (
        0.5
        * (jnp.sign(first_diff) + jnp.sign(second_diff))
        * jnp.minimum(jnp.abs(first_diff), jnp.abs(second_diff))
    )


def take_range(values, start_at, stop_at, along):
    return lax.slice_in_dim(values, start_at, stop_at, axis=along)


def side_terms(values, normal_field):
    density, normal_speed, trans_speed, other_speed, pressure = (
        values[0],
        values[1],
        values[2],
        values[3],
        values[4],
    )
    trans_field, other_field = (values[6], values[7])
    field_sq = normal_field * normal_field + trans_field * trans_field + other_field * other_field
    total_press = pressure + 0.5 * field_sq
    energy = (
        pressure / (GAMMA_RATIO - 1.0)
        + 0.5
        * density
        * (normal_speed * normal_speed + trans_speed * trans_speed + other_speed * other_speed)
        + 0.5 * field_sq
    )
    field_work = normal_speed * normal_field + trans_speed * trans_field + other_speed * other_field
    conserved = (
        density,
        density * normal_speed,
        density * trans_speed,
        density * other_speed,
        energy,
        normal_field,
        trans_field,
        other_field,
    )
    fluxes = (
        density * normal_speed,
        density * normal_speed * normal_speed + total_press - normal_field * normal_field,
        density * normal_speed * trans_speed - normal_field * trans_field,
        density * normal_speed * other_speed - normal_field * other_field,
        (energy + total_press) * normal_speed - normal_field * field_work,
        jnp.zeros_like(density),
        trans_field * normal_speed - normal_field * trans_speed,
        other_field * normal_speed - normal_field * other_speed,
    )
    signal = fast_speed(density, pressure, normal_field, field_sq)
    return (conserved, fluxes, total_press, energy, field_work, signal)


def star_state(values, energy, total_press, field_work, normal_field, outer, middle, star_press):
    density, normal_speed, trans_speed, other_speed = (values[0], values[1], values[2], values[3])
    trans_field, other_field = (values[6], values[7])
    relative = outer - normal_speed
    distance = outer - middle
    star_density = density * relative / distance
    product = density * relative * distance
    divisor = jnp.maximum(product - normal_field * normal_field, 0.5 * product)
    trans_star = trans_speed - normal_field * trans_field * (middle - normal_speed) / divisor
    other_star = other_speed - normal_field * other_field * (middle - normal_speed) / divisor
    factor = (density * relative * relative - normal_field * normal_field) / divisor
    trans_bstar = trans_field * factor
    other_bstar = other_field * factor
    star_work = middle * normal_field + trans_star * trans_bstar + other_star * other_bstar
    star_energy = (
        relative * energy
        - total_press * normal_speed
        + star_press * middle
        + normal_field * (field_work - star_work)
    ) / distance
    return (star_density, trans_star, other_star, trans_bstar, other_bstar, star_work, star_energy)


def hlld_flux(left_values, right_values):
    normal_field = 0.5 * (left_values[5] + right_values[5])
    cons_left, flux_left, press_left, energy_left, work_left, signal_left = side_terms(
        left_values, normal_field
    )
    cons_right, flux_right, press_right, energy_right, work_right, signal_right = side_terms(
        right_values, normal_field
    )
    fastest = jnp.maximum(signal_left, signal_right)
    lower = jnp.minimum(left_values[1], right_values[1]) - fastest
    upper = jnp.maximum(left_values[1], right_values[1]) + fastest
    mass_left = left_values[0] * (lower - left_values[1])
    mass_right = right_values[0] * (upper - right_values[1])
    guess = (
        mass_right * right_values[1] - mass_left * left_values[1] - press_right + press_left
    ) / (mass_right - mass_left)
    margin = 0.1 * (upper - lower)
    middle = jnp.clip(guess, lower + margin, upper - margin)
    star_press = press_left + mass_left * (middle - left_values[1])
    dens_left, trans_left, other_left, tfield_left, ofield_left, swork_left, senergy_left = (
        star_state(
            left_values, energy_left, press_left, work_left, normal_field, lower, middle, star_press
        )
    )
    dens_right, trans_right, other_right, tfield_right, ofield_right, swork_right, senergy_right = (
        star_state(
            right_values,
            energy_right,
            press_right,
            work_right,
            normal_field,
            upper,
            middle,
            star_press,
        )
    )
    root_left = jnp.sqrt(dens_left)
    root_right = jnp.sqrt(dens_right)
    sign_field = jnp.sign(normal_field)
    root_sum = root_left + root_right
    trans_double = (
        root_left * trans_left
        + root_right * trans_right
        + (tfield_right - tfield_left) * sign_field
    ) / root_sum
    other_double = (
        root_left * other_left
        + root_right * other_right
        + (ofield_right - ofield_left) * sign_field
    ) / root_sum
    tfield_double = (
        root_left * tfield_right
        + root_right * tfield_left
        + root_left * root_right * (trans_right - trans_left) * sign_field
    ) / root_sum
    ofield_double = (
        root_left * ofield_right
        + root_right * ofield_left
        + root_left * root_right * (other_right - other_left) * sign_field
    ) / root_sum
    double_work = (
        middle * normal_field + trans_double * tfield_double + other_double * ofield_double
    )
    denergy_left = senergy_left - root_left * (swork_left - double_work) * sign_field
    denergy_right = senergy_right + root_right * (swork_right - double_work) * sign_field
    inner_left = middle - jnp.abs(normal_field) / root_left
    inner_right = middle + jnp.abs(normal_field) / root_right
    star_cons_left = (
        dens_left,
        dens_left * middle,
        dens_left * trans_left,
        dens_left * other_left,
        senergy_left,
        normal_field,
        tfield_left,
        ofield_left,
    )
    star_cons_right = (
        dens_right,
        dens_right * middle,
        dens_right * trans_right,
        dens_right * other_right,
        senergy_right,
        normal_field,
        tfield_right,
        ofield_right,
    )
    double_cons_left = (
        dens_left,
        dens_left * middle,
        dens_left * trans_double,
        dens_left * other_double,
        denergy_left,
        normal_field,
        tfield_double,
        ofield_double,
    )
    double_cons_right = (
        dens_right,
        dens_right * middle,
        dens_right * trans_double,
        dens_right * other_double,
        denergy_right,
        normal_field,
        tfield_double,
        ofield_double,
    )
    outcome = []
    for component in range(8):
        star_left = flux_left[component] + lower * (
            star_cons_left[component] - cons_left[component]
        )
        double_left = star_left + inner_left * (
            double_cons_left[component] - star_cons_left[component]
        )
        star_right = flux_right[component] + upper * (
            star_cons_right[component] - cons_right[component]
        )
        double_right = star_right + inner_right * (
            double_cons_right[component] - star_cons_right[component]
        )
        chosen = jnp.where(
            lower > 0,
            flux_left[component],
            jnp.where(
                inner_left > 0,
                star_left,
                jnp.where(
                    middle > 0,
                    double_left,
                    jnp.where(
                        inner_right > 0,
                        double_right,
                        jnp.where(upper > 0, star_right, flux_right[component]),
                    ),
                ),
            ),
        )
        outcome.append(chosen)
    outcome[5] = jnp.zeros_like(outcome[0])
    return outcome


def direction_divergence(primitives, along, normal_order):
    mapping = (
        0,
        normal_order[0],
        normal_order[1],
        normal_order[2],
        4,
        normal_order[0] + 4,
        normal_order[1] + 4,
        normal_order[2] + 4,
    )
    left_faces = []
    right_faces = []
    for component in range(8):
        values = primitives[mapping[component]]
        length = values.shape[along]
        cell_count = length - 4
        differences = take_range(values, 1, length, along) - take_range(
            values, 0, length - 1, along
        )
        slopes = minmod(
            take_range(differences, 0, length - 2, along),
            take_range(differences, 1, length - 1, along),
        )
        centres = take_range(values, 1, length - 1, along)
        left_faces.append(
            take_range(centres, 0, cell_count + 1, along)
            + 0.5 * take_range(slopes, 0, cell_count + 1, along)
        )
        right_faces.append(
            take_range(centres, 1, cell_count + 2, along)
            - 0.5 * take_range(slopes, 1, cell_count + 2, along)
        )
    face_fluxes = hlld_flux(left_faces, right_faces)
    result = [None] * 8
    for component in range(8):
        face_values = face_fluxes[component]
        length = face_values.shape[along]
        result[mapping[component]] = take_range(face_values, 1, length, along) - take_range(
            face_values, 0, length - 1, along
        )
    return result


def advance(radial_padded, azimuthal_padded, remapped, time_step):
    radial_div = direction_divergence(primitive(radial_padded), 0, (1, 2, 3))
    azimuthal_div = direction_divergence(primitive(azimuthal_padded), 1, (2, 3, 1))
    vertical_padded = jnp.concatenate([remapped[..., -2:], remapped, remapped[..., :2]], axis=3)
    vertical_div = direction_divergence(primitive(vertical_padded), 2, (3, 1, 2))
    gains = [
        0.0,
        2.0 * OMEGA_RATE * remapped[2],
        -(2.0 - SHEAR_RATE) * OMEGA_RATE * remapped[1],
        0.0,
        SHEAR_RATE
        * OMEGA_RATE
        * (remapped[1] * remapped[2] / remapped[0] - remapped[5] * remapped[6]),
        0.0,
        -SHEAR_RATE * OMEGA_RATE * remapped[5],
        0.0,
    ]
    outcome = []
    for component in range(8):
        change = radial_div[component] + azimuthal_div[component] + vertical_div[component]
        outcome.append(remapped[component] - time_step * change + time_step * gains[component])
    return jnp.stack(outcome)


def rotate(blocks, shifts, loop_cells):
    cell_width = blocks.shape[2]
    amount = jnp.mod(shifts, loop_cells)
    whole_part = amount // cell_width
    remainder = amount - whole_part * cell_width
    for bit_index in range(lax.axis_size(AZ).bit_length() - 1):
        shifted = passed_along(blocks, AZ, 1 << bit_index)
        chosen = jnp.bitwise_and(jnp.right_shift(whole_part, bit_index), 1) == 1
        blocks = jnp.where(chosen[None, :, None, None], shifted, blocks)
    before = passed_along(blocks, AZ, 1)
    joined = jnp.concatenate([before, blocks], axis=2)
    positions = cell_width + jnp.arange(cell_width, dtype=jnp.int32)[None, :] - remainder[:, None]
    return jnp.take_along_axis(joined, positions[None, :, :, None], axis=2)


def radial_rim(blocks):
    return padded(blocks, ((RAD, 1),), 2)


def local(fields, offsets, boundary_shift):
    row_count = fields.shape[1]
    cell_width = fields.shape[2]
    loop_cells = cell_width * lax.axis_size(AZ)
    radial_cells = row_count * lax.axis_size(RAD)
    local_peak = jnp.max(cell_speed(primitive(fields)))
    global_peak = one_axis_at_a_time(local_peak, AZ_RAD)
    time_step = CFL_NUMBER / global_peak
    radial_index = lax.axis_index(RAD)
    first_row = radial_index * row_count
    shear_cells = boundary_shift[0]
    extended = radial_rim(fields)
    global_rows = first_row - 2 + jnp.arange(row_count + 4, dtype=jnp.int32)
    source_rows = jnp.mod(global_rows, radial_cells)
    boundary_extra = jnp.where(global_rows < 0, shear_cells, 0) - jnp.where(
        global_rows >= radial_cells, shear_cells, 0
    )
    radial_padded = rotate(extended, jnp.take(offsets, source_rows) + boundary_extra, loop_cells)
    remapped = radial_padded[:, 2 : row_count + 2]
    azimuthal_padded = padded(remapped, ((AZ, 2),), 2)
    return advance(radial_padded, azimuthal_padded, remapped, time_step)


def solution(mesh):
    split = Mesh(mesh.devices.reshape(8, 2, 4, 2, 2), ("az_0", "az_1", "rad_0", "rad_1", "rad_2"))
    return jax.shard_map(
        local,
        mesh=split,
        in_specs=(P(None, RAD, AZ, None), P(), P()),
        out_specs=P(None, RAD, AZ, None),
        check_vma=False,
    )
```

profile of v0, /device:TPU:1, one launch (start us, length us, event | category | flops | bytes accessed | tf_op | source)
XLA Modules:
  0.0 559.9 jit_solution(2137081240276886802)
XLA Ops:
  0.0 1.2 fusion.408
  1.4 2.7 collective-permute-start
  4.2 0.7 collective-permute-start.1
  4.9 2.5 collective-permute-done
  7.4 0.7 constant_dynamic-update-slice_fusion.2
  8.1 3.0 constant_dynamic-update-slice_fusion.1
  11.1 1.1 collective-permute-done.1
  12.2 0.7 constant_dynamic-update-slice_fusion
  12.9 2.4 collective-permute-start.2
  16.1 0.7 gather_fusion
  16.8 57.5 %collective-permute-done.2 = f32[8,20,32,128]{3,0,2,1:T(8,128)} collective-permute-done((f32[8,20,32,128]{3,0,2,1:T(8,128)}, f32[8,20,32,128]{3,0,2,1:T(8,128)}, u32[]{:S(2)}, u32[]{:S(2)}) %collective-permute-start.2) | collective-permute-done | bytes 2621472 | tf_op jit(solution)/shard_map/ppermute | solution.py:20
  74.3 2.9 broadcast_select_fusion
  77.4 55.2 %collective-permute-done.3 = f32[8,20,32,128]{3,0,2,1:T(8,128)S(1)} collective-permute-done((f32[8,20,32,128]{3,0,2,1:T(8,128)S(1)}, f32[8,20,32,128]{3,0,2,1:T(8,128)S(1)}, u32[]{:S(2)}, u32[]{:S(2)}) %collective-permute-start.3) | collective-permute-done | bytes 2621472 | tf_op jit(solution)/shard_map/ppermute | solution.py:20
  132.5 0.4 broadcast_select_fusion.1
  133.0 73.3 %collective-permute-done.4 = f32[8,20,32,128]{3,0,2,1:T(8,128)S(1)} collective-permute-done((f32[8,20,32,128]{3,0,2,1:T(8,128)S(1)}, f32[8,20,32,128]{3,0,2,1:T(8,128)S(1)}, u32[]{:S(2)}, u32[]{:S(2)}) %collective-permute-start.4) | collective-permute-done | bytes 2621472 | tf_op jit(solution)/shard_map/ppermute | solution.py:20
  206.8 5.2 collective-permute-start.5
  212.0 64.0 %collective-permute-done.5 = f32[8,20,32,128]{3,0,2,1:T(8,128)S(1)} collective-permute-done((f32[8,20,32,128]{3,0,2,1:T(8,128)S(1)}, f32[8,20,32,128]{3,0,2,1:T(8,128)S(1)}, u32[]{:S(2)}, u32[]{:S(2)}) %collective-permute-start.5) | collective-permute-done | bytes 2621472 | tf_op jit(solution)/shard_map/ppermute | solution.py:20
  275.9 1.9 broadcast_select_fusion.3
  277.8 6.3 %collective-permute-start.6 = (f32[8,20,32,128]{3,0,2,1:T(8,128)}, f32[8,20,32,128]{3,0,2,1:T(8,128)}, u32[]{:S(2)}, u32[]{:S(2)}) collective-permute-start(f32[8,20,32,128]{3,0,2,1:T(8,128)} %broadcast_select_fusion.3), channel_id=1, source_target_pairs={{0,16},{16,32},{32,48},{48,64},{64,80},{80,96},{96,112},{112,128},... | collective-permute-start | bytes 7864328 | tf_op jit(solution)/shard_map/ppermute | solution.py:20
  284.1 1.5 add_reduce_fusion
  285.6 126.3 %pmax.35 = f32[]{:T(128)} all-reduce(f32[]{:T(128)} %add_reduce_fusion), channel_id=1, replica_groups=mesh['az_0'=8,'az_1'=2,'rad_0'=4,'rad_1'=2,'rad_2'=2] {'az_0'}, use_global_device_ids=true, to_apply=%region_1.0 | all-reduce | flops 1 | bytes 8 | tf_op jit(solution)/shard_map/pmax | solution.py:39
  411.9 55.7 %pmax.36 = f32[]{:T(128)} all-reduce(f32[]{:T(128)} %pmax.35), channel_id=1, replica_groups=mesh['az_0'=8,'az_1'=2,'rad_0'=4,'rad_1'=2,'rad_2'=2] {'az_1'}, use_global_device_ids=true, to_apply=%region_2.0 | all-reduce | flops 1 | bytes 8 | tf_op jit(solution)/shard_map/pmax | solution.py:39
  467.6 9.7 %pmax.37 = f32[]{:T(128)} all-reduce(f32[]{:T(128)} %pmax.36), channel_id=1, replica_groups=mesh['az_0'=8,'az_1'=2,'rad_0'=4,'rad_1'=2,'rad_2'=2] {'rad_0'}, use_global_device_ids=true, to_apply=%region_3.0 | all-reduce | flops 1 | bytes 8 | tf_op jit(solution)/shard_map/pmax | solution.py:39
  477.3 4.4 pmax.38
  481.7 11.5 %pmax.39 = f32[]{:T(128)} all-reduce(f32[]{:T(128)} %pmax.38), channel_id=1, replica_groups=mesh['az_0'=8,'az_1'=2,'rad_0'=4,'rad_1'=2,'rad_2'=2] {'rad_2'}, use_global_device_ids=true, to_apply=%region_5.0 | all-reduce | flops 1 | bytes 8 | tf_op jit(solution)/shard_map/pmax | solution.py:39
  494.1 5.4 pad_maximum_fusion
  499.5 5.9 %gather_fusion.1 = f32[640,8,128]{2,1,0:T(8,128)S(1)} fusion(f32[8,20,64,128]{3,0,2,1:T(8,128)} %pad_maximum_fusion, s32[640]{0:T(1024)S(1)} %reshape.459), kind=kCustom, calls=%fused_computation.1 | custom fusion | bytes 5248000 | tf_op jit(solution)/shard_map/jit(take_along_axis)/gather | solution.py:388
  505.4 0.7 fusion
  506.9 0.8 fusion.407
  507.7 1.7 pad_maximum_fusion.1
  509.6 0.7 fusion.41
  513.9 0.5 minimum_multiply_fusion
  514.9 4.7 select_select_fusion
  519.6 2.8 select_select_fusion.2
  522.3 4.3 fusion.17
  526.6 3.0 select_select_fusion.1
  529.7 3.3 collective-permute-start.7
  533.0 1.8 collective-permute-start.8
  536.0 2.4 select_select_fusion.10
  538.4 1.5 select_select_fusion.11
  539.9 2.2 fusion.192
  542.0 1.4 select_select_fusion.12
  546.5 3.1 select_select_fusion.5
  549.6 1.7 select_select_fusion.7
  551.3 2.9 fusion.102
  554.2 1.8 select_select_fusion.6
  557.3 1.3 copy-done.3
  558.6 0.8 fusion.300
  (69 shorter events, 11.4 us)
Async XLA Ops:
  0.0 16.0 %copy-start = (s32[256]{0:T(256)S(1)}, s32[256]{0:T(256)}, u32[]{:S(2)}) copy-start(s32[256]{0:T(256)} %param.4) | copy-start | bytes 3076
  0.0 8.1 %copy-start.2 = (f32[8,16,32,128]{3,2,1,0:T(8,128)S(1)}, f32[8,16,32,128]{3,2,1,0:T(8,128)}, u32[]{:S(2)}) copy-start(f32[8,16,32,128]{3,2,1,0:T(8,128)} %param.3) | copy-start | bytes 6291460
  1.4 6.0 %collective-permute-start = (f32[8,2,32,128]{3,0,2,1:T(8,128)S(1)}, f32[8,2,32,128]{3,0,2,1:T(8,128)S(1)}, u32[]{:S(2)}, u32[]{:S(2)}) collective-permute-start(f32[8,2,32,128]{3,0,2,1:T(8,128)S(1)} %copy.12), channel_id=1, source_target_pairs={{0,1},{1,2},{2,3},{3,4},{4,5},{5,6},{6,7},{7,8},{8,9},{9,10},{10,1... | collective-permute-start | bytes 786440 | tf_op jit(solution)/shard_map/ppermute | solution.py:29
  4.2 8.0 %collective-permute-start.1 = (f32[8,2,32,128]{3,0,2,1:T(8,128)S(1)}, f32[8,2,32,128]{3,0,2,1:T(8,128)S(1)}, u32[]{:S(2)}, u32[]{:S(2)}) collective-permute-start(f32[8,2,32,128]{3,0,2,1:T(8,128)S(1)} %copy.13), channel_id=1, source_target_pairs={{1,0},{2,1},{3,2},{4,3},{5,4},{6,5},{7,6},{8,7},{9,8},{10,9},{11,1... | collective-permute-start | bytes 786440 | tf_op jit(solution)/shard_map/ppermute | solution.py:32
  12.9 61.4 %collective-permute-start.2 = (f32[8,20,32,128]{3,0,2,1:T(8,128)}, f32[8,20,32,128]{3,0,2,1:T(8,128)}, u32[]{:S(2)}, u32[]{:S(2)}) collective-permute-start(f32[8,20,32,128]{3,0,2,1:T(8,128)} %constant_dynamic-update-slice_fusion), channel_id=1, source_target_pairs={{0,16},{16,32},{32,48},{48,64},{64,80},{80,96},{96,112},{112,128},... | collective-permute-start | bytes 7864328 | tf_op jit(solution)/shard_map/ppermute | solution.py:20
  77.3 55.3 %collective-permute-start.3 = (f32[8,20,32,128]{3,0,2,1:T(8,128)S(1)}, f32[8,20,32,128]{3,0,2,1:T(8,128)S(1)}, u32[]{:S(2)}, u32[]{:S(2)}) collective-permute-start(f32[8,20,32,128]{3,0,2,1:T(8,128)S(1)} %broadcast_select_fusion), channel_id=1, source_target_pairs={{0,32},{16,48},{32,64},{48,80},{64,96},{80,112},{96,128},{112,144}... | collective-permute-start | bytes 7864328 | tf_op jit(solution)/shard_map/ppermute | solution.py:20
  132.9 73.4 %collective-permute-start.4 = (f32[8,20,32,128]{3,0,2,1:T(8,128)S(1)}, f32[8,20,32,128]{3,0,2,1:T(8,128)S(1)}, u32[]{:S(2)}, u32[]{:S(2)}) collective-permute-start(f32[8,20,32,128]{3,0,2,1:T(8,128)S(1)} %broadcast_select_fusion.1), channel_id=1, source_target_pairs={{0,64},{16,80},{32,96},{48,112},{64,128},{80,144},{96,160},{112,17... | collective-permute-start | bytes 7864328 | tf_op jit(solution)/shard_map/ppermute | solution.py:20
  206.8 69.2 %collective-permute-start.5 = (f32[8,20,32,128]{3,0,2,1:T(8,128)S(1)}, f32[8,20,32,128]{3,0,2,1:T(8,128)S(1)}, u32[]{:S(2)}, u32[]{:S(2)}) collective-permute-start(f32[8,20,32,128]{3,0,2,1:T(8,128)S(1)} %broadcast_select_fusion.2), channel_id=1, source_target_pairs={{0,128},{16,144},{32,160},{48,176},{64,192},{80,208},{96,224},{112... | collective-permute-start | bytes 7864328 | tf_op jit(solution)/shard_map/ppermute | solution.py:20
  277.8 216.3 %collective-permute-start.6 = (f32[8,20,32,128]{3,0,2,1:T(8,128)}, f32[8,20,32,128]{3,0,2,1:T(8,128)}, u32[]{:S(2)}, u32[]{:S(2)}) collective-permute-start(f32[8,20,32,128]{3,0,2,1:T(8,128)} %broadcast_select_fusion.3), channel_id=1, source_target_pairs={{0,16},{16,32},{32,48},{48,64},{64,80},{80,96},{96,112},{112,128},... | collective-permute-start | bytes 7864328 | tf_op jit(solution)/shard_map/ppermute | solution.py:20
  529.7 13.8 %collective-permute-start.7 = (f32[8,16,2,128]{3,2,1,0:T(2,128)S(1)}, f32[8,16,2,128]{3,2,1,0:T(2,128)S(1)}, u32[]{:S(2)}, u32[]{:S(2)}) collective-permute-start(f32[8,16,2,128]{3,2,1,0:T(2,128)S(1)} %get-tuple-element.84), channel_id=1, source_target_pairs={{0,16},{16,32},{32,48},{48,64},{64,80},{80,96},{96,112},{112,128},... | collective-permute-start | bytes 393224 | tf_op jit(solution)/shard_map/ppermute | solution.py:29
  533.0 10.5 %collective-permute-start.8 = (f32[8,16,2,128]{3,2,1,0:T(2,128)S(1)}, f32[8,16,2,128]{3,2,1,0:T(2,128)S(1)}, u32[]{:S(2)}, u32[]{:S(2)}) collective-permute-start(f32[8,16,2,128]{3,2,1,0:T(2,128)S(1)} %get-tuple-element.85), channel_id=1, source_target_pairs={{16,0},{32,16},{48,32},{64,48},{80,64},{96,80},{112,96},{128,112},... | collective-permute-start | bytes 393224 | tf_op jit(solution)/shard_map/ppermute | solution.py:32
  556.7 2.7 copy-start.1
  557.3 1.3 copy-start.3
where the time goes:
time: 567 us; the launch traced here: 560 us
  waiting for transfers between devices  254 us (45%)
  blocking collectives  208 us (37%)
  other arithmetic  58.3 us (10%)
  starting transfers between devices  22.6 us (4%)
  local copies, waits for them, and re-layouts  15.4 us (3%)
    ppermute x5, waiting for transfers between devices, passed_along(): lax.ppermute(array, axis, [(i, (i + by) % devices) for i in range(devices)])  250 us
    pmax x5, blocking collectives, one_axis_at_a_time(): array = lax.pmax(array, axis)  208 us
    select_n x12, other arithmetic, hlld_flux(): jnp.where(lower > 0, flux_left[component], jnp.where(inner_left > 0, star...  31.8 us
    ppermute x5, starting transfers between devices, passed_along(): lax.ppermute(array, axis, [(i, (i + by) % devices) for i in range(devices)])  14.1 us
  transfers between devices with their start and end apart: 9, of which 6 were waited for; matrix products, arithmetic and copies ran while one was open for 3% of the time, Pallas kernels for 0%

commit v1 on v0

v1 whole, which is shorter than its diff:
```python
import functools

import jax
import jax.numpy as jnp
from jax import lax
from jax.experimental import pallas as pl
from jax.experimental.pallas import tpu as pltpu
from jax.sharding import Mesh
from jax.sharding import PartitionSpec as P

AZ = ("az_0", "az_1")
RAD = ("rad_0", "rad_1", "rad_2")

GAMMA = 5.0 / 3.0
CFL_NUMBER = 0.4
OMEGA = 1.0
SHEAR = 1.5

FIELDS = 8
ROWS = 16
CELLS = 32
RING = 512
DEPTH = 128
GROUPS = 16
HOLDERS = 16
UNITS = 8
PAIRS = (0, 7, 1, 6, 2, 5, 3, 4)
EXTRA = UNITS * CELLS
PEAK = EXTRA + CELLS
LINES = PEAK + 8
TINY = 1e-30
VMEM = pl.BlockSpec(memory_space=pltpu.VMEM)
SMEM = pl.BlockSpec(memory_space=pltpu.SMEM)
HBM = pl.BlockSpec(memory_space=pl.ANY)
MIB = 1024 * 1024


def passed_along(array, axis, by):
    devices = lax.axis_size(axis)
    return lax.ppermute(array, axis, [(i, (i + by) % devices) for i in range(devices)])


def to_primitive(state):
    density = state[0]
    inverse = 1.0 / density
    vx = state[1] * inverse
    vy = state[2] * inverse
    vz = state[3] * inverse
    kinetic = 0.5 * (state[1] * vx + state[2] * vy + state[3] * vz)
    magnetic = 0.5 * (state[5] * state[5] + state[6] * state[6] + state[7] * state[7])
    pressure = (GAMMA - 1.0) * (state[4] - kinetic - magnetic)
    return (density, vx, vy, vz, pressure, state[5], state[6], state[7])


def fast_speed(density, pressure, normal_field, field_sq):
    sound = (GAMMA * pressure + field_sq) / density
    spread = jnp.maximum(
        sound * sound
        - 4.0 * GAMMA * pressure * normal_field * normal_field / (density * density),
        0.0,
    )
    return jnp.sqrt(0.5 * (sound + jnp.sqrt(spread)))


def cell_speed(prim):
    field_sq = prim[5] * prim[5] + prim[6] * prim[6] + prim[7] * prim[7]
    total = jnp.abs(prim[1]) + fast_speed(prim[0], prim[4], prim[5], field_sq)
    total = total + jnp.abs(prim[2]) + fast_speed(prim[0], prim[4], prim[6], field_sq)
    return total + jnp.abs(prim[3]) + fast_speed(prim[0], prim[4], prim[7], field_sq)


def half_slope(before, after):
    return 0.5 * jnp.minimum(
        jnp.maximum(after, jnp.minimum(before, 0.0)), jnp.maximum(before, 0.0)
    )


def hlld(left, right):
    rl, ul, tl, wl, pl_, nl, btl, bwl = left
    rr, ur, tr, wr, pr_, nr, btr, bwr = right
    bn = 0.5 * (nl + nr)
    bn2 = bn * bn

    def signal(p, bt, bw):
        b2 = bn2 + bt * bt + bw * bw
        gp = GAMMA * p
        h = gp + b2
        square = jnp.maximum(h * h - 4.0 * (gp * bn2), TINY)
        return h + square * lax.rsqrt(square), p + 0.5 * b2

    sig_l, ptl = signal(pl_, btl, bwl)
    sig_r, ptr = signal(pr_, btr, bwr)
    inv_rr = 1.0 / (rl * rr)
    square = (0.5 * inv_rr) * jnp.maximum(sig_l * rr, sig_r * rl)
    fastest = square * lax.rsqrt(square)
    lower = jnp.minimum(ul, ur) - fastest
    upper = jnp.maximum(ul, ur) + fastest
    rel_l = lower - ul
    rel_r = upper - ur
    ml = rl * rel_l
    mr = rr * rel_r
    guess = (mr * ur - ml * ul - ptr + ptl) / (mr - ml)
    margin = 0.1 * (upper - lower)
    sm = jnp.minimum(jnp.maximum(guess, lower + margin), upper - margin)
    press_star = ptl + ml * (sm - ul)

    def star(m, rel, outer, u, t, w, bt, bw):
        dist = outer - sm
        inv_dist = 1.0 / dist
        product = m * dist
        inv_div = 1.0 / jnp.maximum(product - bn2, 0.5 * product)
        k = bn * (sm - u) * inv_div
        factor = (m * rel - bn2) * inv_div
        dens = m * inv_dist
        inv_root = lax.rsqrt(dens)
        return (inv_dist, dens, dens * inv_root, inv_root,
                t - bt * k, w - bw * k, bt * factor, bw * factor)

    idl, dl, ql, iql, tsl, wsl, btsl, bwsl = star(ml, rel_l, lower, ul, tl, wl, btl, bwl)
    idr, dr, qr, iqr, tsr, wsr, btsr, bwsr = star(mr, rel_r, upper, ur, tr, wr, btr, bwr)
    sg = jnp.where(bn < 0.0, -1.0, 1.0)
    inv_sum = 1.0 / (ql + qr)
    al = ql * inv_sum
    ar = qr * inv_sum
    sgs = sg * inv_sum
    qqs = ql * ar * sg
    t2 = al * tsl + ar * tsr + (btsr - btsl) * sgs
    w2 = al * wsl + ar * wsr + (bwsr - bwsl) * sgs
    bt2 = al * btsr + ar * btsl + qqs * (tsr - tsl)
    bw2 = al * bwsr + ar * bwsl + qqs * (wsr - wsl)

    pos = sm > 0.0

    def pick(a, b):
        return jnp.where(pos, a, b)

    r, u, t, w, p = pick(rl, rr), pick(ul, ur), pick(tl, tr), pick(wl, wr), pick(pl_, pr_)
    bt, bw, pt, outer = pick(btl, btr), pick(bwl, bwr), pick(ptl, ptr), pick(lower, upper)
    rel, inv_dist, dens = pick(rel_l, rel_r), pick(idl, idr), pick(dl, dr)
    ts, ws, bts, bws = pick(tsl, tsr), pick(wsl, wsr), pick(btsl, btsr), pick(bwsl, bwsr)
    bn_abs = bn * sg
    root_s = pick(-ql, qr)
    inner = sm + bn_abs * pick(-iql, iqr)
    zero = jnp.zeros_like(sm)
    inner_pos = inner > 0.0
    lower_pos = lower > 0.0
    dbl = jnp.where(pos, jnp.where(lower_pos | inner_pos, zero, inner),
                    jnp.where(inner_pos, inner, zero))
    s = jnp.where(pos, jnp.where(lower_pos, zero, lower),
                  jnp.where(inner_pos | (upper > 0.0), upper, zero))

    ru = r * u
    energy = p * (1.0 / (GAMMA - 1.0)) + 0.5 * (ru * u + r * (t * t + w * w)) + (pt - p)
    vb = u * bn + t * bt + w * bw
    sb = sm * bn
    work = sb + ts * bts + ws * bws
    work2 = sb + t2 * bt2 + w2 * bw2
    energy_star = (rel * energy - pt * u + press_star * sm + bn * (vb - work)) * inv_dist
    dd = dbl * dens
    sd = s * dens
    sr = s * r
    f_r = ru + (sd - sr)
    f_n = ru * u + pt - bn2 + (sd * sm - sr * u)
    f_t = ru * t - bn * bt + (sd * ts - sr * t) + dd * (t2 - ts)
    f_w = ru * w - bn * bw + (sd * ws - sr * w) + dd * (w2 - ws)
    f_e = ((energy + pt) * u - bn * vb + s * (energy_star - energy)
           + dbl * (root_s * sg * (work - work2)))
    f_bt = bt * u - bn * t + s * (bts - bt) + dbl * (bt2 - bts)
    f_bw = bw * u - bn * w + s * (bws - bw) + dbl * (bw2 - bws)
    return (f_r, f_n, f_t, f_w, f_e, f_bt, f_bw)


def order_of(normal):
    n = normal
    t = n % 3 + 1
    w = t % 3 + 1
    return (0, n, t, w, 4, n + 4, t + 4, w + 4)


def flux_slots(normal):
    o = order_of(normal)
    return (o[0], o[1], o[2], o[3], o[4], o[6], o[7])


def params(mib):
    return pltpu.CompilerParams(vmem_limit_bytes=mib * MIB)


def pack(fields):
    def kernel(fields_ref, units_ref, stage_ref, in_sems, out_sems):
        arriving = []
        for u, pair in enumerate(PAIRS):
            copy = pltpu.make_async_copy(
                fields_ref.at[:, pl.ds(2 * pair, 2)], stage_ref.at[u], in_sems.at[u])
            copy.start()
            arriving.append(copy)
        leaving = []
        for u, pair in enumerate(PAIRS):
            arriving[u].wait()
            for f in range(FIELDS):
                h = (2 * pair + 2 * f) % HOLDERS
                copy = pltpu.make_async_copy(
                    stage_ref.at[u, f], units_ref.at[pl.ds(h, 2), u],
                    out_sems.at[u * FIELDS + f])
                copy.start()
                leaving.append(copy)
        for copy in leaving:
            copy.wait()

    return pl.pallas_call(
        kernel,
        out_shape=jax.ShapeDtypeStruct((HOLDERS, UNITS, CELLS, DEPTH), jnp.float32),
        in_specs=[HBM],
        out_specs=HBM,
        scratch_shapes=[
            pltpu.VMEM((UNITS, FIELDS, 2, CELLS, DEPTH), jnp.float32),
            pltpu.SemaphoreType.DMA((UNITS,)),
            pltpu.SemaphoreType.DMA((UNITS * FIELDS,)),
        ],
        name="pack",
    )(fields)


def rotate_rings(pos, offsets, shift, rings, peak):
    blocks = RING // CELLS

    def kernel(pos_ref, offsets_ref, shift_ref, peak_ref, ring_ref, out_ref, wide_ref):
        parity = pos_ref[0] & 1
        group = pos_ref[1]
        shear = shift_ref[0]

        def send(unit, slot, amount):
            for b in range(blocks):
                wide_ref[slot, b * CELLS:(b + 1) * CELLS, :] = ring_ref[b, unit]
            wide_ref[slot, RING:RING + CELLS, :] = ring_ref[0, unit]
            wide_ref[slot, RING + CELLS:, :] = ring_ref[1, unit, 0:8]
            low = (-amount) & 7
            for b in range(blocks):
                base = pl.multiple_of(((b * CELLS - amount) & (RING - 1)) - low, 8)
                block = wide_ref[slot, pl.ds(base, CELLS + 8), :]
                block = pltpu.roll(block, CELLS + 8 - low, 0)
                out_ref[b, slot * CELLS:(slot + 1) * CELLS, :] = block[0:CELLS]

        def amount_of(row):
            return offsets_ref[group * ROWS + row]

        for unit, pair in enumerate(PAIRS):
            send(unit, unit, amount_of(2 * pair + parity))
        last = group == GROUPS - 1
        row = jnp.where(last, ROWS - 2, 0) + parity
        send(jnp.where(last, 1, 0), UNITS, amount_of(row) + jnp.where(last, shear, -shear))
        for b in range(blocks):
            out_ref[b, PEAK:, :] = peak_ref[...]

    return pl.pallas_call(
        kernel,
        out_shape=jax.ShapeDtypeStruct((blocks, LINES, DEPTH), jnp.float32),
        in_specs=[SMEM, SMEM, SMEM, VMEM, VMEM],
        out_specs=VMEM,
        scratch_shapes=[pltpu.VMEM((UNITS + 1, RING + CELLS + 8, DEPTH), jnp.float32)],
        compiler_params=params(16),
        name="rotate",
    )(pos, offsets, shift, peak, rings)


def rims(pos, blocks):
    ghost = jax.ShapeDtypeStruct((FIELDS, 2, CELLS, DEPTH), jnp.float32)
    edge = jax.ShapeDtypeStruct((FIELDS, ROWS, 2, DEPTH), jnp.float32)

    def kernel(pos_ref, blocks_ref, left_ref, right_ref, up_ref, down_ref):
        group = pos_ref[1]
        top_at = pl.multiple_of(jnp.where(group == GROUPS - 1, EXTRA, CELLS), 8)
        low_at = pl.multiple_of(jnp.where(group == 0, EXTRA, 0), 8)
        for f in range(FIELDS):
            for u, pair in enumerate(PAIRS):
                for r in range(2):
                    h = (2 * pair + r + 2 * f) % HOLDERS
                    right_ref[f, 2 * pair + r] = blocks_ref[
                        h, (u + 1) * CELLS - 2:(u + 1) * CELLS, :]
                    left_ref[f, 2 * pair + r] = blocks_ref[h, u * CELLS:u * CELLS + 2, :]
            for r in range(2):
                top = (ROWS - 2 + r + 2 * f) % HOLDERS
                low = (r + 2 * f) % HOLDERS
                up_ref[f, r] = blocks_ref[top, pl.ds(top_at, CELLS), :]
                down_ref[f, r] = blocks_ref[low, pl.ds(low_at, CELLS), :]

    return pl.pallas_call(
        kernel,
        out_shape=(edge, edge, ghost, ghost),
        in_specs=[SMEM, VMEM],
        out_specs=(VMEM,) * 4,
        compiler_params=params(8),
        name="rims",
    )(pos, blocks)


PAD = 8
WIDE = 48
Z_BLOCK = 32
Z_UNROLL = 4
S_UNROLL = 2
R_BLOCK = 16
A_BLOCK = 16


def unit_of(row):
    pair = row >> 1
    return jnp.where(pair < 4, 2 * pair, 15 - 2 * pair)


def load(blocks_ref, row, start, size):
    at = pl.multiple_of(unit_of(row) * CELLS + start, 8)
    return [blocks_ref[(row + 2 * f) & (HOLDERS - 1), pl.ds(at, size), :]
            for f in range(FIELDS)]


def vertical(blocks, first, rows):
    order = order_of(3)
    slots = flux_slots(3)
    parts = CELLS // Z_BLOCK

    def kernel(blocks_ref, acc_ref, left_ref, right_ref, flux_ref):
        def states(r, carry):
            prim = to_primitive(load(blocks_ref, first + r, 0, CELLS))
            for k, f in enumerate(order):
                value = prim[f]
                below = pltpu.roll(value, 1, 1)
                above = pltpu.roll(value, DEPTH - 1, 1)
                beyond = pltpu.roll(value, DEPTH - 2, 1)
                step = above - value
                left_ref[k, r] = value + half_slope(value - below, step)
                right_ref[k, r] = above - half_slope(step, beyond - above)
            return carry

        lax.fori_loop(0, rows, states, 0, unroll=S_UNROLL)

        def fluxes(n, carry):
            r = n // parts if parts > 1 else n
            at = pl.ds(pl.multiple_of((n % parts if parts > 1 else 0) * Z_BLOCK, 8), Z_BLOCK)
            flux = hlld([left_ref[k, r, at, :] for k in range(8)],
                        [right_ref[k, r, at, :] for k in range(8)])
            for k in range(7):
                flux_ref[k, r, at, :] = flux[k]
            return carry

        lax.fori_loop(0, rows * parts, fluxes, 0)

        def changes(r, carry):
            state = load(blocks_ref, first + r, 0, CELLS)
            gains = [
                None,
                2.0 * OMEGA * state[2],
                -(2.0 - SHEAR) * OMEGA * state[1],
                None,
                SHEAR * OMEGA * (state[1] * state[2] / state[0] - state[5] * state[6]),
                None,
                -SHEAR * OMEGA * state[5],
                None,
            ]
            for k, slot in enumerate(slots):
                value = flux_ref[k, r]
                change = pltpu.roll(value, 1, 1) - value
                if gains[slot] is not None:
                    change = change + gains[slot]
                acc_ref[slot, r] = change
            return carry

        lax.fori_loop(0, rows, changes, 0, unroll=Z_UNROLL)

    sides = pltpu.VMEM((8, rows, CELLS, DEPTH), jnp.float32)
    return pl.pallas_call(
        kernel,
        out_shape=jax.ShapeDtypeStruct((FIELDS - 1, rows, CELLS, DEPTH), jnp.float32),
        in_specs=[VMEM],
        out_specs=VMEM,
        scratch_shapes=[sides, sides, sides],
        compiler_params=params(16),
        name=f"vertical{first}",
    )(blocks)


def march(order, window, runs):
    def face(at, steps, lefts):
        new_steps, new_lefts, rights = [], [], []
        here, there = window(at), window(at + 1)
        for k, f in enumerate(order):
            step = there[f] - here[f]
            slope = half_slope(steps[k], step)
            rights.append(here[f] - slope)
            new_lefts.append(here[f] + slope)
            new_steps.append(step)
        return hlld(lefts, rights), new_steps, new_lefts

    a, b, c = window(-2), window(-1), window(0)
    steps = [c[f] - b[f] for f in order]
    lefts = [b[f] + half_slope(b[f] - a[f], step) for f, step in zip(order, steps)]
    lower, steps, lefts = face(0, steps, lefts)

    def body(emit, i, carry):
        lower, steps, lefts = carry
        upper, steps, lefts = face(i + 1, steps, lefts)
        emit(i, lower, upper)
        return (upper, steps, lefts)

    carry = (lower, steps, lefts)
    for start, stop, emit in runs:
        carry = lax.fori_loop(start, stop, functools.partial(body, emit), carry)


def finish(blocks, accs, below, above, before, after):
    def kernel(blocks_ref, acc0_ref, acc1_ref, below_ref, above_ref, before_ref, after_ref,
               out_ref, prim_ref, turn_ref):
        def put(values, row, start, size):
            for f in range(FIELDS):
                prim_ref[f, pl.ds(pl.multiple_of(row * WIDE, 8) + start, size), :] = values[f]

        def fill(i, carry):
            put(to_primitive(load(blocks_ref, i, 0, CELLS)), i + 2, PAD, CELLS)
            put(to_primitive([before_ref[f, i] for f in range(FIELDS)]), i + 2, PAD - 2, 2)
            put(to_primitive([after_ref[f, i] for f in range(FIELDS)]), i + 2, PAD + CELLS, 2)
            return carry

        lax.fori_loop(0, ROWS, fill, 0)
        for r in range(2):
            put(to_primitive([below_ref[f, r] for f in range(FIELDS)]), r, PAD, CELLS)
            put(to_primitive([above_ref[f, r] for f in range(FIELDS)]), ROWS + 2 + r, PAD, CELLS)

        for start in range(0, ROWS, A_BLOCK):
            def rows_at(a):
                return [jnp.concatenate([
                    prim_ref[f, pl.ds((start + g + 2) * WIDE + PAD + a, 8, stride=WIDE), :]
                    for g in range(0, A_BLOCK, 8)], axis=0) for f in range(FIELDS)]

            def keep(a, lower, upper):
                at = pl.ds(pl.multiple_of(a * ROWS, 8) + start, A_BLOCK)
                for k in range(7):
                    turn_ref[k, at, :] = lower[k] - upper[k]

            march(order_of(2), rows_at, [(0, CELLS, keep)])

        a_slots = flux_slots(2)
        slots = flux_slots(1)
        peak = blocks_ref[0, PEAK:, :]
        for b in range(1, HOLDERS):
            peak = jnp.maximum(peak, blocks_ref[b, PEAK:, :])
        dt = CFL_NUMBER / peak[0:1]

        for start in range(0, CELLS, R_BLOCK):
            part = slice(start, start + R_BLOCK)

            def cells_at(i):
                at = pl.multiple_of((i + 2) * WIDE, 8) + PAD + start
                return [prim_ref[f, pl.ds(at, R_BLOCK), :] for f in range(FIELDS)]

            def update(acc_ref, first, i, lower, upper):
                state = load(blocks_ref, i, start, R_BLOCK)
                change = [None] * FIELDS
                for k, slot in enumerate(slots):
                    change[slot] = lower[k] - upper[k]
                for k, slot in enumerate(a_slots):
                    turn = jnp.concatenate([
                        turn_ref[k, pl.ds((start + g) * ROWS + i, 8, stride=ROWS), :]
                        for g in range(0, R_BLOCK, 8)], axis=0)
                    change[slot] = turn if change[slot] is None else change[slot] + turn
                for slot in range(FIELDS - 1):
                    total = acc_ref[slot, i - first, part, :]
                    total = total if change[slot] is None else total + change[slot]
                    out_ref[slot, i, part, :] = state[slot] + dt * total
                out_ref[7, i, part, :] = state[7] + dt * change[7]

            half = ROWS // 2
            march(order_of(1), cells_at, [
                (0, half, functools.partial(update, acc0_ref, 0)),
                (half, ROWS, functools.partial(update, acc1_ref, half))])

    return pl.pallas_call(
        kernel,
        out_shape=jax.ShapeDtypeStruct((FIELDS, ROWS, CELLS, DEPTH), jnp.float32),
        in_specs=[VMEM] * 7,
        out_specs=VMEM,
        scratch_shapes=[
            pltpu.VMEM((FIELDS, (ROWS + 4) * WIDE, DEPTH), jnp.float32),
            pltpu.VMEM((7, CELLS * ROWS, DEPTH), jnp.float32),
        ],
        compiler_params=params(24),
        name="finish",
    )(blocks, *accs, below, above, before, after)


def over(peak, axis):
    for by in (1, 2, 4, 8):
        peak = jnp.maximum(peak, passed_along(peak, axis, by))
    return peak


def exchanged(units):
    return lax.all_to_all(units, AZ, split_axis=0, concat_axis=0, tiled=True)


def local(fields, offsets, boundary_shift):
    pos = jnp.stack([lax.axis_index(AZ), lax.axis_index(RAD)]).astype(jnp.int32)
    rings = exchanged(pack(fields))
    peak = jnp.broadcast_to(jnp.max(cell_speed(to_primitive(fields))), (8, DEPTH))
    peak = over(peak, RAD)
    blocks = exchanged(rotate_rings(pos, offsets, boundary_shift, rings, peak))
    left, right, up, down = rims(pos, blocks)
    acc0 = vertical(blocks, 0, ROWS // 2)
    acc0, left, right, up, down = lax.optimization_barrier((acc0, left, right, up, down))
    below = passed_along(up, RAD, 1)
    above = passed_along(down, RAD, -1)
    before = passed_along(right, AZ, 1)
    after = passed_along(left, AZ, -1)
    acc1 = vertical(blocks, ROWS // 2, ROWS // 2)
    return finish(blocks, (acc0, acc1), below, above, before, after)


def solution(mesh):
    split = Mesh(mesh.devices.reshape(8, 2, 4, 2, 2), ("az_0", "az_1", "rad_0", "rad_1", "rad_2"))
    return jax.shard_map(
        local,
        mesh=split,
        in_specs=(P(None, RAD, AZ, None), P(), P()),
        out_specs=P(None, RAD, AZ, None),
        check_vma=False,
    )
```

time: 567 us -> 160 us (0.28)
  waiting for transfers between devices: 254 us -> 43.8 us
  blocking collectives: 208 us -> 64 us
  other arithmetic: 58.3 us -> 4.33 us
  Pallas kernels: 0 us -> 21.4 us
  local copies, waits for them, and re-layouts: 15.4 us -> 0.63 us
    ppermute x5 -> x8, waiting for transfers between devices: 250 us -> 14 us  [passed_along(): lax.ppermute(array, axis, [(i, (i + by) % devices) for i in range(devices)])]
    pmax x5 -> x0, blocking collectives: 208 us -> none  [one_axis_at_a_time(): array = lax.pmax(array, axis)]
    all_to_all x0 -> x1, blocking collectives: none -> 64 us  [exchanged(): return lax.all_to_all(units, AZ, split_axis=0, concat_axis=0, tiled=True)]
    select_n x18 -> x0, other arithmetic: 38.1 us -> none  [the longest x12 31.8 us: hlld_flux(): jnp.where(lower > 0, flux_left[component], jnp.where(inner_left > 0, star...]
    all_to_all x0 -> x1, waiting for transfers between devices: none -> 29.8 us  [exchanged(): return lax.all_to_all(units, AZ, split_axis=0, concat_axis=0, tiled=True)]
    pallas_call x0 -> x6, Pallas kernels: none -> 21.4 us  [the longest x1 10.9 us: finish(): pl.pallas_call(kernel, out_shape=jax.ShapeDtypeStruct((FIELDS, ROWS, CELL...]
    all_to_all x0 -> x1, starting transfers between devices: none -> 11.6 us  [exchanged(): return lax.all_to_all(units, AZ, split_axis=0, concat_axis=0, tiled=True)]
    ppermute x4 -> x0, starting transfers between devices: 8.53 us -> none  [the longest x2 6.01 us: padded(): lax.ppermute(lax.slice_in_dim(block, block.shape[dim] - width, None, axis...]
  transfers between devices with their start and end apart: 9 -> 9, of which waited for: 6 -> 7; matrix products, arithmetic and copies ran while one was open for 3% -> 3% of each run, Pallas kernels for 0% -> 2%
where the time goes in v1:
time: 160 us; the launch traced here: 158 us
  blocking collectives  64 us (40%)
  waiting for transfers between devices  43.8 us (27%)
  starting transfers between devices  23.1 us (14%)
  Pallas kernels  21.4 us (13%)
  other arithmetic  4.33 us (3%)
    all_to_all x1, blocking collectives, exchanged(): return lax.all_to_all(units, AZ, split_axis=0, concat_axis=0, tiled=True)  64 us
    all_to_all x1, waiting for transfers between devices, exchanged(): return lax.all_to_all(units, AZ, split_axis=0, concat_axis=0, tiled=True)  29.8 us
    ppermute x8, waiting for transfers between devices, passed_along(): lax.ppermute(array, axis, [(i, (i + by) % devices) for i in range(devices)])  14 us
    all_to_all x1, starting transfers between devices, exchanged(): return lax.all_to_all(units, AZ, split_axis=0, concat_axis=0, tiled=True)  11.6 us
    ppermute x8, starting transfers between devices, passed_along(): lax.ppermute(array, axis, [(i, (i + by) % devices) for i in range(devices)])  11.6 us
    pallas_call x1, Pallas kernels, finish(): pl.pallas_call(kernel, out_shape=jax.ShapeDtypeStruct((FIELDS, ROWS, CELL...  10.9 us
    pallas_call x2, Pallas kernels, vertical(): pl.pallas_call(kernel, out_shape=jax.ShapeDtypeStruct((FIELDS - 1, rows,...  5.67 us
  transfers between devices with their start and end apart: 9, of which 7 were waited for; matrix products, arithmetic and copies ran while one was open for 3% of the time, Pallas kernels for 2%

profile of v1, /device:TPU:1, one launch (start us, length us, event | category | flops | bytes accessed | tf_op | source)
XLA Modules:
  0.0 158.0 jit_solution(3392135673620266066)
XLA Ops:
  0.0 2.9 %pack.1 = f32[16,8,32,128]{3,2,1,0:T(8,128)} custom-call(f32[8,16,32,128]{3,2,1,0:T(8,128)} %fields_ref.1), custom_call_target="tpu_custom_call" | custom-call | tf_op jit(solution)/shard_map/pack/pallas_call | solution.py:210
  2.9 11.6 %all-to-all-start = ((f32[16,8,32,128]{3,2,1,0:T(8,128)}), f32[16,8,32,128]{3,2,1,0:T(8,128)S(1)}, u32[]{:S(2)}, u32[]{:S(2)}) async-start(f32[16,8,32,128]{3,2,1,0:T(8,128)} %pack.1), calls=%async_computation | async-start | bytes 4194304 | tf_op jit(solution)/shard_map/all_to_all | solution.py:497
  14.5 0.0 copy-start
  14.5 3.0 %add_reduce_fusion = f32[]{:T(128)} fusion(f32[8,16,32,128]{3,2,1,0:T(8,128)} %fields_ref.1), kind=kLoop, calls=%fused_computation.40 | loop fusion | flops 3538943 | bytes 2097156 | tf_op jit(solution)/shard_map/reduce_max | solution.py:503
  17.5 0.6 broadcast_in_dim.3
  18.1 1.2 collective-permute-start
  19.3 0.8 collective-permute-done
  20.1 0.6 broadcast_maximum_fusion
  20.7 2.2 %collective-permute-start.1 = (f32[8,128]{1,0:T(8,128)S(1)}, f32[8,128]{1,0:T(8,128)S(1)}, u32[]{:S(2)}, u32[]{:S(2)}) collective-permute-start(f32[8,128]{1,0:T(8,128)S(1)} %broadcast_maximum_fusion), channel_id=1, source_target_pairs={{0,2},{1,3},{2,4},{3,5},{4,6},{5,7},{6,8},{7,9},{8,10},{9,11},{10,... | collective-permute-start | bytes 12296 | tf_op jit(solution)/shard_map/ppermute | solution.py:40
  23.0 2.7 %collective-permute-done.1 = f32[8,128]{1,0:T(8,128)S(1)} collective-permute-done((f32[8,128]{1,0:T(8,128)S(1)}, f32[8,128]{1,0:T(8,128)S(1)}, u32[]{:S(2)}, u32[]{:S(2)}) %collective-permute-start.1) | collective-permute-done | bytes 4128 | tf_op jit(solution)/shard_map/ppermute | solution.py:40
  25.7 0.6 fusion.25
  26.3 0.2 collective-permute-start.2
  26.5 3.9 %collective-permute-done.2 = f32[8,128]{1,0:T(8,128)S(1)} collective-permute-done((f32[8,128]{1,0:T(8,128)S(1)}, f32[8,128]{1,0:T(8,128)S(1)}, u32[]{:S(2)}, u32[]{:S(2)}) %collective-permute-start.2) | collective-permute-done | bytes 4128 | tf_op jit(solution)/shard_map/ppermute | solution.py:40
  30.4 0.5 collective-permute-start.3
  30.9 0.1 pad_add_fusion.pos_ref
  31.6 3.0 %collective-permute-done.3 = f32[8,128]{1,0:T(8,128)S(1)} collective-permute-done((f32[8,128]{1,0:T(8,128)S(1)}, f32[8,128]{1,0:T(8,128)S(1)}, u32[]{:S(2)}, u32[]{:S(2)}) %collective-permute-start.3) | collective-permute-done | bytes 4128 | tf_op jit(solution)/shard_map/ppermute | solution.py:40
  34.6 29.8 %all-to-all-done.ring_ref = f32[16,8,32,128]{3,2,1,0:T(8,128)S(1)} async-done(((f32[16,8,32,128]{3,2,1,0:T(8,128)}), f32[16,8,32,128]{3,2,1,0:T(8,128)S(1)}, u32[]{:S(2)}, u32[]{:S(2)}) %all-to-all-start) | async-done | bytes 2097184 | tf_op jit(solution)/shard_map/all_to_all | solution.py:497
  64.4 0.0 copy-done
  64.4 1.2 rotate.1
  65.6 64.0 %all_to_all.10.blocks_ref = f32[16,296,128]{2,1,0:T(8,128)S(1)} all-to-all(f32[16,296,128]{2,1,0:T(8,128)S(1)} %rotate.1), channel_id=1, replica_groups=mesh['az_0'=8,'az_1'=2,'rad_0'=4,'rad_1'=2,'rad_2'=2] {'az_0','az_1'}, dimensions={0} | all-to-all | bytes 4849664 | tf_op jit(solution)/shard_map/all_to_all | solution.py:497
  129.7 0.7 rims.1
  130.4 2.8 %vertical0.1.acc0_ref = f32[7,8,32,128]{3,2,1,0:T(8,128)S(1)} custom-call(f32[16,296,128]{2,1,0:T(8,128)S(1)} %all_to_all.10.blocks_ref), custom_call_target="tpu_custom_call" | custom-call | tf_op jit(solution)/shard_map/vertical0/pallas_call | solution.py:371
  133.2 2.3 %collective-permute-start.4 = (f32[8,2,32,128]{3,2,1,0:T(8,128)S(1)}, f32[8,2,32,128]{3,2,1,0:T(8,128)S(1)}, u32[]{:S(2)}, u32[]{:S(2)}) collective-permute-start(f32[8,2,32,128]{3,2,1,0:T(8,128)S(1)} %get-tuple-element.19), channel_id=1, source_target_pairs={{0,1},{1,2},{2,3},{3,4},{4,5},{5,6},{6,7},{7,8},{8,9},{9,10},{10,1... | collective-permute-start | bytes 786440 | tf_op jit(solution)/shard_map/ppermute | solution.py:40
  135.5 0.0 collective-permute-start.5
  135.5 0.8 collective-permute-start.6
  136.3 4.3 %collective-permute-start.7 = (f32[8,16,2,128]{3,2,1,0:T(2,128)S(1)}, f32[8,16,2,128]{3,2,1,0:T(2,128)S(1)}, u32[]{:S(2)}, u32[]{:S(2)}) collective-permute-start(f32[8,16,2,128]{3,2,1,0:T(2,128)S(1)} %get-tuple-element.22), channel_id=1, source_target_pairs={{0,240},{16,0},{32,16},{48,32},{64,48},{80,64},{96,80},{112,96},{1... | collective-permute-start | bytes 393224 | tf_op jit(solution)/shard_map/ppermute | solution.py:40
  140.6 2.8 %vertical8.1.acc1_ref = f32[7,8,32,128]{3,2,1,0:T(8,128)S(1)} custom-call(f32[16,296,128]{2,1,0:T(8,128)S(1)} %all_to_all.10.blocks_ref), custom_call_target="tpu_custom_call" | custom-call | tf_op jit(solution)/shard_map/vertical8/pallas_call | solution.py:371
  143.5 0.0 collective-permute-done.6.before_ref
  143.5 1.0 collective-permute-done.7.after_ref
  144.5 0.0 collective-permute-done.4.below_ref
  144.5 2.6 %collective-permute-done.5.above_ref = f32[8,2,32,128]{3,2,1,0:T(8,128)S(1)} collective-permute-done((f32[8,2,32,128]{3,2,1,0:T(8,128)S(1)}, f32[8,2,32,128]{3,2,1,0:T(8,128)S(1)}, u32[]{:S(2)}, u32[]{:S(2)}) %collective-permute-start.5) | collective-permute-done | bytes 262176 | tf_op jit(solution)/shard_map/ppermute | solution.py:40
  147.1 10.9 %finish.1 = f32[8,16,32,128]{3,2,1,0:T(8,128)} custom-call(f32[16,296,128]{2,1,0:T(8,128)S(1)} %all_to_all.10.blocks_ref, f32[7,8,32,128]{3,2,1,0:T(8,128)S(1)} %vertical0.1.acc0_ref, f32[7,8,32,128]{3,2,1,0:T(8,128)S(1)} %vertical8.1.acc1_ref, f32[8,2,32,128]{3,2,1,0:T(8,128)S(1)} %collective-permute-done.4.below_ref, ...), custom_call_target="tpu_custom_call" | custom-call | tf_op jit(solution)/shard_map/finish/pallas_call | solution.py:476
  (2 shorter events, 0.0 us)
Async XLA Ops:
  2.9 61.5 %all-to-all-start = ((f32[16,8,32,128]{3,2,1,0:T(8,128)}), f32[16,8,32,128]{3,2,1,0:T(8,128)S(1)}, u32[]{:S(2)}, u32[]{:S(2)}) async-start(f32[16,8,32,128]{3,2,1,0:T(8,128)} %pack.1), calls=%async_computation | async-start | bytes 4194304 | tf_op jit(solution)/shard_map/all_to_all | solution.py:497
  14.5 49.9 %copy-start = (s32[256]{0:T(256)S(1)}, s32[256]{0:T(256)}, u32[]{:S(2)}) copy-start(s32[256]{0:T(256)} %offsets_ref.1) | copy-start | bytes 3076
  18.1 2.0 %collective-permute-start = (f32[8,128]{1,0:T(8,128)S(1)}, f32[8,128]{1,0:T(8,128)S(1)}, u32[]{:S(2)}, u32[]{:S(2)}) collective-permute-start(f32[8,128]{1,0:T(8,128)S(1)} %broadcast_in_dim.3), channel_id=1, source_target_pairs={{0,1},{1,2},{2,3},{3,4},{4,5},{5,6},{6,7},{7,8},{8,9},{9,10},{10,1... | collective-permute-start | bytes 12296 | tf_op jit(solution)/shard_map/ppermute | solution.py:40
  20.7 4.9 %collective-permute-start.1 = (f32[8,128]{1,0:T(8,128)S(1)}, f32[8,128]{1,0:T(8,128)S(1)}, u32[]{:S(2)}, u32[]{:S(2)}) collective-permute-start(f32[8,128]{1,0:T(8,128)S(1)} %broadcast_maximum_fusion), channel_id=1, source_target_pairs={{0,2},{1,3},{2,4},{3,5},{4,6},{5,7},{6,8},{7,9},{8,10},{9,11},{10,... | collective-permute-start | bytes 12296 | tf_op jit(solution)/shard_map/ppermute | solution.py:40
  26.3 4.1 %collective-permute-start.2 = (f32[8,128]{1,0:T(8,128)S(1)}, f32[8,128]{1,0:T(8,128)S(1)}, u32[]{:S(2)}, u32[]{:S(2)}) collective-permute-start(f32[8,128]{1,0:T(8,128)S(1)} %fusion.25), channel_id=1, source_target_pairs={{0,4},{1,5},{2,6},{3,7},{4,8},{5,9},{6,10},{7,11},{8,12},{9,13},{1... | collective-permute-start | bytes 12296 | tf_op jit(solution)/shard_map/ppermute | solution.py:40
  30.4 4.3 %collective-permute-start.3 = (f32[8,128]{1,0:T(8,128)S(1)}, f32[8,128]{1,0:T(8,128)S(1)}, u32[]{:S(2)}, u32[]{:S(2)}) collective-permute-start(f32[8,128]{1,0:T(8,128)S(1)} %max.26), channel_id=1, source_target_pairs={{0,8},{1,9},{2,10},{3,11},{4,12},{5,13},{6,14},{7,15},{8,0},{9,1},... | collective-permute-start | bytes 12296 | tf_op jit(solution)/shard_map/ppermute | solution.py:40
  133.2 11.3 %collective-permute-start.4 = (f32[8,2,32,128]{3,2,1,0:T(8,128)S(1)}, f32[8,2,32,128]{3,2,1,0:T(8,128)S(1)}, u32[]{:S(2)}, u32[]{:S(2)}) collective-permute-start(f32[8,2,32,128]{3,2,1,0:T(8,128)S(1)} %get-tuple-element.19), channel_id=1, source_target_pairs={{0,1},{1,2},{2,3},{3,4},{4,5},{5,6},{6,7},{7,8},{8,9},{9,10},{10,1... | collective-permute-start | bytes 786440 | tf_op jit(solution)/shard_map/ppermute | solution.py:40
  135.5 11.6 %collective-permute-start.5 = (f32[8,2,32,128]{3,2,1,0:T(8,128)S(1)}, f32[8,2,32,128]{3,2,1,0:T(8,128)S(1)}, u32[]{:S(2)}, u32[]{:S(2)}) collective-permute-start(f32[8,2,32,128]{3,2,1,0:T(8,128)S(1)} %get-tuple-element.20), channel_id=1, source_target_pairs={{0,15},{1,0},{2,1},{3,2},{4,3},{5,4},{6,5},{7,6},{8,7},{9,8},{10,9... | collective-permute-start | bytes 786440 | tf_op jit(solution)/shard_map/ppermute | solution.py:40
  135.5 7.9 %collective-permute-start.6 = (f32[8,16,2,128]{3,2,1,0:T(2,128)S(1)}, f32[8,16,2,128]{3,2,1,0:T(2,128)S(1)}, u32[]{:S(2)}, u32[]{:S(2)}) collective-permute-start(f32[8,16,2,128]{3,2,1,0:T(2,128)S(1)} %get-tuple-element.21), channel_id=1, source_target_pairs={{0,16},{16,32},{32,48},{48,64},{64,80},{80,96},{96,112},{112,128},... | collective-permute-start | bytes 393224 | tf_op jit(solution)/shard_map/ppermute | solution.py:40
  136.3 8.2 %collective-permute-start.7 = (f32[8,16,2,128]{3,2,1,0:T(2,128)S(1)}, f32[8,16,2,128]{3,2,1,0:T(2,128)S(1)}, u32[]{:S(2)}, u32[]{:S(2)}) collective-permute-start(f32[8,16,2,128]{3,2,1,0:T(2,128)S(1)} %get-tuple-element.22), channel_id=1, source_target_pairs={{0,240},{16,0},{32,16},{48,32},{64,48},{80,64},{96,80},{112,96},{1... | collective-permute-start | bytes 393224 | tf_op jit(solution)/shard_map/ppermute | solution.py:40

commit v2 on v1

v2 whole, which is shorter than its diff:
```python
import functools

import jax
import jax.numpy as jnp
from jax import lax
from jax.experimental import pallas as pl
from jax.experimental.pallas import tpu as pltpu
from jax.sharding import PartitionSpec as P


AZ = "az"
RAD = "rad"

GAMMA = 5.0 / 3.0
CFL_NUMBER = 0.4
OMEGA = 1.0
SHEAR = 1.5

FIELDS = 8
ROWS = 16
CELLS = 32
RING = 512
DEPTH = 128
GROUPS = 16
HOLDERS = 16
UNITS = 8
PAIRS = (0, 7, 1, 6, 2, 5, 3, 4)
EXTRA = UNITS * CELLS
LINES = EXTRA + CELLS
GHOSTS = FIELDS * 2 * CELLS
ORDER = tuple(2 * z + x for x in (0, 1) for z in (0, 7, 1, 6, 2, 5, 3, 4))
BACK = ORDER[::-1]
PLACE = tuple(ORDER.index(d) for d in range(HOLDERS))
HOLDER = tuple(BACK.index(d) for d in range(HOLDERS))
TINY = 1e-30
VMEM = pl.BlockSpec(memory_space=pltpu.VMEM)
SMEM = pl.BlockSpec(memory_space=pltpu.SMEM)
HBM = pl.BlockSpec(memory_space=pl.ANY)
MIB = 1024 * 1024


def passed_along(array, axis, by):
    devices = lax.axis_size(axis)
    return lax.ppermute(array, axis, [(i, (i + by) % devices) for i in range(devices)])


def to_primitive(state):
    density = state[0]
    inverse = 1.0 / density
    vx = state[1] * inverse
    vy = state[2] * inverse
    vz = state[3] * inverse
    kinetic = 0.5 * (state[1] * vx + state[2] * vy + state[3] * vz)
    magnetic = 0.5 * (state[5] * state[5] + state[6] * state[6] + state[7] * state[7])
    pressure = (GAMMA - 1.0) * (state[4] - kinetic - magnetic)
    return (density, vx, vy, vz, pressure, state[5], state[6], state[7])


def fast_speed(density, pressure, normal_field, field_sq):
    sound = (GAMMA * pressure + field_sq) / density
    spread = jnp.maximum(
        sound * sound
        - 4.0 * GAMMA * pressure * normal_field * normal_field / (density * density),
        0.0,
    )
    return jnp.sqrt(0.5 * (sound + jnp.sqrt(spread)))


def cell_speed(prim):
    field_sq = prim[5] * prim[5] + prim[6] * prim[6] + prim[7] * prim[7]
    total = jnp.abs(prim[1]) + fast_speed(prim[0], prim[4], prim[5], field_sq)
    total = total + jnp.abs(prim[2]) + fast_speed(prim[0], prim[4], prim[6], field_sq)
    return total + jnp.abs(prim[3]) + fast_speed(prim[0], prim[4], prim[7], field_sq)


def half_slope(before, after):
    return 0.5 * jnp.minimum(
        jnp.maximum(after, jnp.minimum(before, 0.0)), jnp.maximum(before, 0.0)
    )


def hlld(left, right):
    rl, ul, tl, wl, pl_, nl, btl, bwl = left
    rr, ur, tr, wr, pr_, nr, btr, bwr = right
    bn = 0.5 * (nl + nr)
    bn2 = bn * bn
    bn2_4 = (4.0 * GAMMA) * bn2

    def signal(r, p, bt, bw):
        b2 = bn2 + (bt * bt + bw * bw)
        h = GAMMA * p + b2
        square = jnp.maximum(h * h - p * bn2_4, TINY)
        return (h + square * lax.rsqrt(square)) * (1.0 / r), p + 0.5 * b2

    sig_l, ptl = signal(rl, pl_, btl, bwl)
    sig_r, ptr = signal(rr, pr_, btr, bwr)
    square = 0.5 * jnp.maximum(sig_l, sig_r)
    fastest = square * lax.rsqrt(square)
    lower = jnp.minimum(ul, ur) - fastest
    upper = jnp.maximum(ul, ur) + fastest
    rel_l = lower - ul
    rel_r = upper - ur
    ml = rl * rel_l
    mr = rr * rel_r
    guess = (mr * ur - ml * ul - ptr + ptl) * (1.0 / (mr - ml))
    margin = 0.1 * (upper - lower)
    sm = jnp.minimum(jnp.maximum(guess, lower + margin), upper - margin)
    press_star = ptl + ml * (sm - ul)

    def star(m, rel, outer, u, t, w, bt, bw):
        dist = outer - sm
        product = m * dist
        inv_div = 1.0 / jnp.maximum(product - bn2, 0.5 * product)
        k = (sm - u) * (bn * inv_div)
        factor = (m * rel - bn2) * inv_div
        dens = m * (1.0 / dist)
        return (dens, dens * lax.rsqrt(dens),
                t - bt * k, w - bw * k, bt * factor, bw * factor)

    dl, ql, tsl, wsl, btsl, bwsl = star(ml, rel_l, lower, ul, tl, wl, btl, bwl)
    dr, qr, tsr, wsr, btsr, bwsr = star(mr, rel_r, upper, ur, tr, wr, btr, bwr)
    inv_sum = 1.0 / (ql + qr)
    al = ql * inv_sum
    ar = qr * inv_sum

    pos = sm > 0.0

    def pick(a, b):
        return jnp.where(pos, a, b)

    sg = jnp.where(bn < 0.0, -1.0, 1.0)
    sgs = sg * inv_sum
    qqs = (ql * qr) * sgs
    side_sg = pick(-sg, sg)
    own, other = pick(ar, -al), pick(al, -ar)
    jump_t, jump_w = tsr - tsl, wsr - wsl
    jump_bt, jump_bw = btsr - btsl, bwsr - bwsl
    more_t = own * jump_t + sgs * jump_bt
    more_w = own * jump_w + sgs * jump_bw
    more_bt = other * jump_bt + qqs * jump_t
    more_bw = other * jump_bw + qqs * jump_w

    r, u, t, w, p = pick(rl, rr), pick(ul, ur), pick(tl, tr), pick(wl, wr), pick(pl_, pr_)
    bt, bw, pt, outer = pick(btl, btr), pick(bwl, bwr), pick(ptl, ptr), pick(lower, upper)
    dens = pick(dl, dr)
    ts, ws, bts, bws = pick(tsl, tsr), pick(wsl, wsr), pick(btsl, btsr), pick(bwsl, bwsr)
    inv_root = lax.rsqrt(dens)
    inner = sm + (bn * side_sg) * inv_root
    inside = jnp.logical_not(lower > 0.0)
    inner_pos = inner > 0.0
    s = jnp.where(inside & (inner_pos | (upper > 0.0)), outer, 0.0)
    dbl = jnp.where(inside & (inner_pos ^ pos), inner, 0.0)

    energy = pt + 0.5 * (p + r * (u * u + t * t + w * w))
    vb = u * bn + t * bt + w * bw
    work = sm * bn + ts * bts + ws * bws
    more_work = (ts * more_bt + more_t * (bts + more_bt)
                 + ws * more_bw + more_w * (bws + more_bw))
    ptu = pt * u
    energy_star = ((outer - u) * energy - ptu + press_star * sm + bn * (vb - work)) * (
        1.0 / (outer - sm))
    us = u - s
    mm = r * us
    sd = s * dens
    dd = dbl * dens
    f_r = mm + sd
    f_n = mm * u + sd * sm + (pt - bn2)
    f_t = mm * t + sd * ts - bn * bt + dd * more_t
    f_w = mm * w + sd * ws - bn * bw + dd * more_w
    f_e = (energy * us + ptu - bn * vb + s * energy_star
           - dbl * ((dens * inv_root) * side_sg * more_work))
    f_bt = bt * us - bn * t + s * bts + dbl * more_bt
    f_bw = bw * us - bn * w + s * bws + dbl * more_bw
    return (f_r, f_n, f_t, f_w, f_e, f_bt, f_bw)


def order_of(normal):
    n = normal
    t = n % 3 + 1
    w = t % 3 + 1
    return (0, n, t, w, 4, n + 4, t + 4, w + 4)


def flux_slots(normal):
    o = order_of(normal)
    return (o[0], o[1], o[2], o[3], o[4], o[6], o[7])


def params(mib):
    return pltpu.CompilerParams(vmem_limit_bytes=mib * MIB)


def pack(fields):
    def kernel(fields_ref, units_ref, stage_ref, in_sems, out_sems):
        arriving = []
        for u, pair in enumerate(PAIRS):
            copy = pltpu.make_async_copy(
                fields_ref.at[:, pl.ds(2 * pair, 2)], stage_ref.at[u], in_sems.at[u])
            copy.start()
            arriving.append(copy)
        leaving = []
        for u, pair in enumerate(PAIRS):
            arriving[u].wait()
            for f in range(FIELDS):
                for r in range(2):
                    place = PLACE[BACK[(2 * pair + r + 2 * f) % HOLDERS]]
                    copy = pltpu.make_async_copy(
                        stage_ref.at[u, f, r], units_ref.at[place, u],
                        out_sems.at[(u * FIELDS + f) * 2 + r])
                    copy.start()
                    leaving.append(copy)
        for copy in leaving:
            copy.wait()

    return pl.pallas_call(
        kernel,
        out_shape=jax.ShapeDtypeStruct((HOLDERS, UNITS, CELLS, DEPTH), jnp.float32),
        in_specs=[HBM],
        out_specs=HBM,
        scratch_shapes=[
            pltpu.VMEM((UNITS, FIELDS, 2, CELLS, DEPTH), jnp.float32),
            pltpu.SemaphoreType.DMA((UNITS,)),
            pltpu.SemaphoreType.DMA((UNITS * FIELDS * 2,)),
        ],
        name="pack",
    )(fields)


def rotate_rings(pos, offsets, shift, rings, peak):
    blocks = RING // CELLS

    def kernel(pos_ref, offsets_ref, shift_ref, peak_ref, ring_ref, out_ref, wide_ref):
        parity = pos_ref[0] & 1
        group = pos_ref[1]
        shear = shift_ref[0]

        def send(unit, slot, amount):
            for b in range(blocks):
                wide_ref[slot, b * CELLS:(b + 1) * CELLS, :] = ring_ref[PLACE[b], unit]
            wide_ref[slot, RING:RING + CELLS, :] = ring_ref[PLACE[0], unit]
            wide_ref[slot, RING + CELLS:, :] = ring_ref[PLACE[1], unit, 0:8]
            low = (-amount) & 7
            for b in range(blocks):
                base = pl.multiple_of(((b * CELLS - amount) & (RING - 1)) - low, 8)
                block = wide_ref[slot, pl.ds(base, CELLS + 8), :]
                block = pltpu.roll(block, CELLS + 8 - low, 0)
                out_ref[HOLDER[b], slot * CELLS:(slot + 1) * CELLS, :] = block[0:CELLS]

        def amount_of(row):
            return offsets_ref[group * ROWS + row]

        for unit, pair in enumerate(PAIRS):
            send(unit, unit, amount_of(2 * pair + parity))
        last = group == GROUPS - 1
        row = jnp.where(last, ROWS - 2, 0) + parity
        send(jnp.where(last, 1, 0), UNITS, amount_of(row) + jnp.where(last, shear, -shear))

        @pl.when((group > 0) & (group < GROUPS - 1))
        def _():
            for b in range(blocks):
                out_ref[b, EXTRA:EXTRA + 8, :] = peak_ref[...]

    return pl.pallas_call(
        kernel,
        out_shape=jax.ShapeDtypeStruct((blocks, LINES, DEPTH), jnp.float32),
        in_specs=[SMEM, SMEM, SMEM, VMEM, VMEM],
        out_specs=VMEM,
        scratch_shapes=[pltpu.VMEM((UNITS + 1, RING + CELLS + 8, DEPTH), jnp.float32)],
        compiler_params=params(16),
        name="rotate",
    )(pos, offsets, shift, peak, rings)


def peak_of(blocks_ref):
    peak = blocks_ref[0, EXTRA:EXTRA + 8, :]
    for h in range(1, HOLDERS):
        peak = jnp.maximum(peak, blocks_ref[h, EXTRA:EXTRA + 8, :])
    return peak


def rims(pos, blocks):
    ghost = jax.ShapeDtypeStruct((GHOSTS + 8, DEPTH), jnp.float32)
    edge = jax.ShapeDtypeStruct((FIELDS, ROWS, 2, DEPTH), jnp.float32)

    def kernel(pos_ref, blocks_ref, left_ref, right_ref, up_ref, down_ref):
        group = pos_ref[1]
        top_at = pl.multiple_of(jnp.where(group == GROUPS - 1, EXTRA, CELLS), 8)
        low_at = pl.multiple_of(jnp.where(group == 0, EXTRA, 0), 8)
        for f in range(FIELDS):
            for u, pair in enumerate(PAIRS):
                for r in range(2):
                    h = (2 * pair + r + 2 * f) % HOLDERS
                    right_ref[f, 2 * pair + r] = blocks_ref[
                        h, (u + 1) * CELLS - 2:(u + 1) * CELLS, :]
                    left_ref[f, 2 * pair + r] = blocks_ref[h, u * CELLS:u * CELLS + 2, :]
            for r in range(2):
                top = (ROWS - 2 + r + 2 * f) % HOLDERS
                low = (r + 2 * f) % HOLDERS
                at = (2 * f + r) * CELLS
                up_ref[at:at + CELLS, :] = blocks_ref[top, pl.ds(top_at, CELLS), :]
                down_ref[at:at + CELLS, :] = blocks_ref[low, pl.ds(low_at, CELLS), :]
        peak = peak_of(blocks_ref)
        up_ref[GHOSTS:, :] = peak
        down_ref[GHOSTS:, :] = peak

    return pl.pallas_call(
        kernel,
        out_shape=(edge, edge, ghost, ghost),
        in_specs=[SMEM, VMEM],
        out_specs=(VMEM,) * 4,
        compiler_params=params(8),
        name="rims",
    )(pos, blocks)


PAD = 8
WIDE = 48
R_BLOCK = CELLS // 2


def unit_of(row):
    pair = row >> 1
    return jnp.where(pair < 4, 2 * pair, 15 - 2 * pair)


def load(blocks_ref, row, start, size):
    at = pl.multiple_of(unit_of(row) * CELLS + start, 8)
    return [blocks_ref[(row + 2 * f) & (HOLDERS - 1), pl.ds(at, size), :]
            for f in range(FIELDS)]


def vertical(blocks, first, rows):
    order = order_of(3)
    slots = flux_slots(3)

    def kernel(blocks_ref, acc_ref, left_ref, right_ref, flux_ref):
        def states(r):
            prim = to_primitive(load(blocks_ref, first + r, 0, CELLS))
            for k, f in enumerate(order):
                value = prim[f]
                below = pltpu.roll(value, 1, 1)
                above = pltpu.roll(value, DEPTH - 1, 1)
                beyond = pltpu.roll(value, DEPTH - 2, 1)
                step = above - value
                left_ref[k, r] = value + half_slope(value - below, step)
                right_ref[k, r] = above - half_slope(step, beyond - above)

        def fluxes(r):
            flux = hlld([left_ref[k, r] for k in range(8)], [right_ref[k, r] for k in range(8)])
            for k in range(7):
                flux_ref[k, r] = flux[k]

        def changes(r):
            state = load(blocks_ref, first + r, 0, CELLS)
            gains = [
                None,
                2.0 * OMEGA * state[2],
                -(2.0 - SHEAR) * OMEGA * state[1],
                None,
                SHEAR * OMEGA * (state[1] * state[2] / state[0] - state[5] * state[6]),
                None,
                -SHEAR * OMEGA * state[5],
                None,
            ]
            for k, slot in enumerate(slots):
                value = flux_ref[k, r]
                change = pltpu.roll(value, 1, 1) - value
                if gains[slot] is not None:
                    change = change + gains[slot]
                acc_ref[slot, r] = change

        states(0)

        def body(r, carry):
            changes(jnp.maximum(r - 1, 0))
            fluxes(r)
            states(jnp.minimum(r + 1, rows - 1))
            return carry

        lax.fori_loop(0, rows, body, 0)
        changes(rows - 1)

    sides = pltpu.VMEM((8, rows, CELLS, DEPTH), jnp.float32)
    return pl.pallas_call(
        kernel,
        out_shape=jax.ShapeDtypeStruct((FIELDS - 1, rows, CELLS, DEPTH), jnp.float32),
        in_specs=[VMEM],
        out_specs=VMEM,
        scratch_shapes=[sides, sides, sides],
        compiler_params=params(16),
    )(blocks)


def march(order, window, runs):
    def face(at, steps, lefts):
        new_steps, new_lefts, rights = [], [], []
        here, there = window(at), window(at + 1)
        for k, f in enumerate(order):
            step = there[f] - here[f]
            slope = half_slope(steps[k], step)
            rights.append(here[f] - slope)
            new_lefts.append(here[f] + slope)
            new_steps.append(step)
        return hlld(lefts, rights), new_steps, new_lefts

    a, b, c = window(-2), window(-1), window(0)
    steps = [c[f] - b[f] for f in order]
    lefts = [b[f] + half_slope(b[f] - a[f], step) for f, step in zip(order, steps)]
    lower, steps, lefts = face(0, steps, lefts)

    def body(emit, i, carry):
        lower, steps, lefts = carry
        upper, steps, lefts = face(i + 1, steps, lefts)
        emit(i, lower, upper)
        return (upper, steps, lefts)

    carry = (lower, steps, lefts)
    for start, stop, emit in runs:
        carry = lax.fori_loop(start, stop, functools.partial(body, emit), carry)


def fill(blocks_ref, prim_ref, top, start, size):
    def body(i, carry):
        values = to_primitive(load(blocks_ref, i, start, size))
        at = pl.multiple_of((i + top) * WIDE, 8) + PAD + start
        for f in range(FIELDS):
            prim_ref[f, pl.ds(at, size), :] = values[f]
        return carry

    lax.fori_loop(0, ROWS, body, 0)


def azimuthal(blocks, edge, half):
    first = half * (CELLS // 2)

    def kernel(blocks_ref, edge_ref, turn_ref, prim_ref):
        fill(blocks_ref, prim_ref, 0, 8 * half, CELLS - 8)
        at = PAD + CELLS if half else PAD - 2

        def sides(i, carry):
            values = to_primitive([edge_ref[f, i] for f in range(FIELDS)])
            for f in range(FIELDS):
                prim_ref[f, pl.ds(pl.multiple_of(i * WIDE, 8) + at, 2), :] = values[f]
            return carry

        lax.fori_loop(0, ROWS, sides, 0, unroll=4)

        def rows_at(a):
            return [jnp.concatenate([
                prim_ref[f, pl.ds(g * WIDE + PAD + first + a, 8, stride=WIDE), :]
                for g in range(0, ROWS, 8)], axis=0) for f in range(FIELDS)]

        def keep(a, lower, upper):
            for k in range(7):
                turn_ref[k, pl.ds(pl.multiple_of(a * ROWS, 8), ROWS), :] = lower[k] - upper[k]

        march(order_of(2), rows_at, [(0, CELLS // 2, keep)])

    return pl.pallas_call(
        kernel,
        out_shape=jax.ShapeDtypeStruct((7, CELLS // 2 * ROWS, DEPTH), jnp.float32),
        in_specs=[VMEM] * 2,
        out_specs=VMEM,
        scratch_shapes=[pltpu.VMEM((FIELDS, ROWS * WIDE, DEPTH), jnp.float32)],
        compiler_params=params(12),
    )(blocks, edge)


def finish(pos, blocks, accs, turns, below, above):
    def kernel(pos_ref, blocks_ref, acc0_ref, acc1_ref, turn0_ref, turn1_ref, below_ref, above_ref,
               out_ref, prim_ref):
        fill(blocks_ref, prim_ref, 2, 0, CELLS)
        for ghost_ref, row in ((below_ref, 0), (above_ref, ROWS + 2)):
            for r in range(2):
                values = to_primitive([
                    ghost_ref[(2 * f + r) * CELLS:(2 * f + r + 1) * CELLS, :]
                    for f in range(FIELDS)])
                at = (row + r) * WIDE + PAD
                for f in range(FIELDS):
                    prim_ref[f, at:at + CELLS, :] = values[f]

        a_slots = flux_slots(2)
        slots = flux_slots(1)
        group = pos_ref[1]
        peak = jnp.where(
            group == 0, above_ref[GHOSTS:, :],
            jnp.where(group == GROUPS - 1, below_ref[GHOSTS:, :], peak_of(blocks_ref)))
        dt = CFL_NUMBER / peak[0:1]

        for start, turn_ref in ((0, turn0_ref), (R_BLOCK, turn1_ref)):
            part = slice(start, start + R_BLOCK)

            def cells_at(i):
                at = pl.multiple_of((i + 2) * WIDE, 8) + PAD + start
                return [prim_ref[f, pl.ds(at, R_BLOCK), :] for f in range(FIELDS)]

            def update(acc_ref, first, i, lower, upper):
                state = load(blocks_ref, i, start, R_BLOCK)
                change = [None] * FIELDS
                for k, slot in enumerate(slots):
                    change[slot] = lower[k] - upper[k]
                for k, slot in enumerate(a_slots):
                    turn = jnp.concatenate([
                        turn_ref[k, pl.ds(g * ROWS + i, 8, stride=ROWS), :]
                        for g in range(0, R_BLOCK, 8)], axis=0)
                    change[slot] = turn if change[slot] is None else change[slot] + turn
                for slot in range(FIELDS - 1):
                    total = acc_ref[slot, i - first, part, :]
                    total = total if change[slot] is None else total + change[slot]
                    out_ref[slot, i, part, :] = state[slot] + dt * total
                out_ref[7, i, part, :] = state[7] + dt * change[7]

            half = ROWS // 2
            march(order_of(1), cells_at, [
                (0, half, functools.partial(update, acc0_ref, 0)),
                (half, ROWS, functools.partial(update, acc1_ref, half))])

    return pl.pallas_call(
        kernel,
        out_shape=jax.ShapeDtypeStruct((FIELDS, ROWS, CELLS, DEPTH), jnp.float32),
        in_specs=[SMEM] + [VMEM] * 7,
        out_specs=VMEM,
        scratch_shapes=[pltpu.VMEM((FIELDS, (ROWS + 4) * WIDE, DEPTH), jnp.float32)],
        compiler_params=params(20),
        name="finish",
    )(pos, blocks, *accs, *turns, below, above)


def over(peak, axis):
    for by in (1, 2, 4, 8):
        peak = jnp.maximum(peak, passed_along(peak, axis, by))
    return peak


def exchanged(units, order):
    return lax.all_to_all(units, AZ, split_axis=0, concat_axis=0, tiled=True,
                          axis_index_groups=[list(order)])


def local(fields, offsets, boundary_shift):
    holder = jnp.take(jnp.array(HOLDER, jnp.int32), lax.axis_index(AZ))
    pos = jnp.stack([holder, lax.axis_index(RAD).astype(jnp.int32)])
    rings = exchanged(pack(fields), ORDER)
    peak = jnp.broadcast_to(jnp.max(cell_speed(to_primitive(fields))), (8, DEPTH))
    peak = over(peak, RAD)
    blocks = exchanged(rotate_rings(pos, offsets, boundary_shift, rings, peak), BACK)
    left, right, up, down = rims(pos, blocks)
    before = passed_along(right, AZ, 1)
    acc0 = vertical(blocks, 0, ROWS // 2)
    acc0, up, blocks = lax.optimization_barrier((acc0, up, blocks))
    below = passed_along(up, RAD, 1)
    acc1 = vertical(blocks, ROWS // 2, ROWS // 2)
    acc1, left, blocks = lax.optimization_barrier((acc1, left, blocks))
    after = passed_along(left, AZ, -1)
    turn0 = azimuthal(blocks, before, 0)
    turn0, down, blocks = lax.optimization_barrier((turn0, down, blocks))
    above = passed_along(down, RAD, -1)
    turn1 = azimuthal(blocks, after, 1)
    return finish(pos, blocks, (acc0, acc1), (turn0, turn1), below, above)


def solution(mesh):
    return jax.shard_map(
        local,
        mesh=mesh,
        in_specs=(P(None, RAD, AZ, None), P(), P()),
        out_specs=P(None, RAD, AZ, None),
        check_vma=False,
    )
```

time: 160 us -> 158 us (0.988)
  the two profiles are of different devices: /device:TPU:1 before, /device:TPU:32 now
where the time goes in v2:
time: 158 us; the launch traced here: 157 us
  blocking collectives  60.9 us (39%)
  waiting for transfers between devices  46.5 us (29%)
  Pallas kernels  23.1 us (15%)
  starting transfers between devices  19.8 us (13%)
  other arithmetic  4.33 us (3%)
    all_to_all x1, blocking collectives, exchanged(): lax.all_to_all(units, AZ, split_axis=0, concat_axis=0, tiled=True, axis_i...  60.9 us
    ppermute x8, waiting for transfers between devices, passed_along(): lax.ppermute(array, axis, [(i, (i + by) % devices) for i in range(devices)])  30.3 us
    all_to_all x1, waiting for transfers between devices, exchanged(): lax.all_to_all(units, AZ, split_axis=0, concat_axis=0, tiled=True, axis_i...  16.3 us
    all_to_all x1, starting transfers between devices, exchanged(): lax.all_to_all(units, AZ, split_axis=0, concat_axis=0, tiled=True, axis_i...  11.1 us
    ppermute x8, starting transfers between devices, passed_along(): lax.ppermute(array, axis, [(i, (i + by) % devices) for i in range(devices)])  8.76 us
    pallas_call x1, Pallas kernels, finish(): pl.pallas_call(kernel, out_shape=jax.ShapeDtypeStruct((FIELDS, ROWS, CELL...  6.73 us
    pallas_call x2, Pallas kernels, azimuthal(): pl.pallas_call(kernel, out_shape=jax.ShapeDtypeStruct((7, CELLS // 2 * RO...  5.62 us
    pallas_call x2, Pallas kernels, vertical(): pl.pallas_call(kernel, out_shape=jax.ShapeDtypeStruct((FIELDS - 1, rows,...  5.4 us
  transfers between devices with their start and end apart: 9, of which 6 were waited for; matrix products, arithmetic and copies ran while one was open for 4% of the time, Pallas kernels for 7%

profile of v2, /device:TPU:32, one launch (start us, length us, event | category | flops | bytes accessed | tf_op | source)
XLA Modules:
  0.0 157.4 jit_solution(15258873744384791743)
XLA Ops:
  0.0 3.4 %pack.1 = f32[16,8,32,128]{3,2,1,0:T(8,128)} custom-call(f32[8,16,32,128]{3,2,1,0:T(8,128)} %fields_ref.1), custom_call_target="tpu_custom_call" | custom-call | tf_op jit(solution)/shard_map/pack/pallas_call | solution.py:215
  3.4 11.1 %all-to-all-start = ((f32[16,8,32,128]{3,2,1,0:T(8,128)}), f32[16,8,32,128]{3,2,1,0:T(8,128)S(1)}, u32[]{:S(2)}, u32[]{:S(2)}) async-start(f32[16,8,32,128]{3,2,1,0:T(8,128)} %pack.1), calls=%async_computation | async-start | bytes 4194304 | tf_op jit(solution)/shard_map/all_to_all | solution.py:536
  14.5 0.0 copy-start.1
  14.5 0.0 copy-start
  14.5 3.0 %add_reduce_fusion = f32[]{:T(128)} fusion(f32[8,16,32,128]{3,2,1,0:T(8,128)} %fields_ref.1), kind=kLoop, calls=%fused_computation.40 | loop fusion | flops 3538943 | bytes 2097156 | tf_op jit(solution)/shard_map/reduce_max | solution.py:544
  17.5 0.6 broadcast_in_dim.8
  18.1 0.1 collective-permute-start
  18.2 5.2 %collective-permute-done = f32[8,128]{1,0:T(8,128)S(1)} collective-permute-done((f32[8,128]{1,0:T(8,128)S(1)}, f32[8,128]{1,0:T(8,128)S(1)}, u32[]{:S(2)}, u32[]{:S(2)}) %collective-permute-start) | collective-permute-done | bytes 4128 | tf_op jit(solution)/shard_map/ppermute | solution.py:44
  23.5 0.6 broadcast_maximum_fusion
  24.1 0.1 collective-permute-start.1
  24.2 11.5 %collective-permute-done.1 = f32[8,128]{1,0:T(8,128)S(1)} collective-permute-done((f32[8,128]{1,0:T(8,128)S(1)}, f32[8,128]{1,0:T(8,128)S(1)}, u32[]{:S(2)}, u32[]{:S(2)}) %collective-permute-start.1) | collective-permute-done | bytes 4128 | tf_op jit(solution)/shard_map/ppermute | solution.py:44
  35.7 0.6 fusion.25
  36.3 0.1 collective-permute-start.2
  36.4 0.0 copy-done.1
  36.4 0.6 dynamic-slice.4
  37.7 3.5 %collective-permute-done.2 = f32[8,128]{1,0:T(8,128)S(1)} collective-permute-done((f32[8,128]{1,0:T(8,128)S(1)}, f32[8,128]{1,0:T(8,128)S(1)}, u32[]{:S(2)}, u32[]{:S(2)}) %collective-permute-start.2) | collective-permute-done | bytes 4128 | tf_op jit(solution)/shard_map/ppermute | solution.py:44
  41.2 0.0 collective-permute-start.3
  41.2 0.1 pad_add_fusion.pos_ref
  42.0 4.4 %collective-permute-done.3 = f32[8,128]{1,0:T(8,128)S(1)} collective-permute-done((f32[8,128]{1,0:T(8,128)S(1)}, f32[8,128]{1,0:T(8,128)S(1)}, u32[]{:S(2)}, u32[]{:S(2)}) %collective-permute-start.3) | collective-permute-done | bytes 4128 | tf_op jit(solution)/shard_map/ppermute | solution.py:44
  46.4 16.3 %all-to-all-done.ring_ref = f32[16,8,32,128]{3,2,1,0:T(8,128)S(1)} async-done(((f32[16,8,32,128]{3,2,1,0:T(8,128)}), f32[16,8,32,128]{3,2,1,0:T(8,128)S(1)}, u32[]{:S(2)}, u32[]{:S(2)}) %all-to-all-start) | async-done | bytes 2097184 | tf_op jit(solution)/shard_map/all_to_all | solution.py:536
  62.6 0.0 copy-done
  62.6 1.2 rotate.1
  63.9 60.9 %all_to_all.10.blocks_ref = f32[16,288,128]{2,1,0:T(8,128)S(1)} all-to-all(f32[16,288,128]{2,1,0:T(8,128)S(1)} %rotate.1), channel_id=1, replica_groups={{144,112,176,80,208,48,240,16,128,96,160,64,192,32,224,0},{145,113,177,..., dimensions={0} | all-to-all | bytes 4718592 | tf_op jit(solution)/shard_map/all_to_all | solution.py:536
  124.8 0.7 rims.1
  125.5 2.2 %collective-permute-start.4 = (f32[8,16,2,128]{3,2,1,0:T(2,128)S(1)}, f32[8,16,2,128]{3,2,1,0:T(2,128)S(1)}, u32[]{:S(2)}, u32[]{:S(2)}) collective-permute-start(f32[8,16,2,128]{3,2,1,0:T(2,128)S(1)} %get-tuple-element.22), channel_id=1, source_target_pairs={{0,16},{16,32},{32,48},{48,64},{64,80},{80,96},{96,112},{112,128},... | collective-permute-start | bytes 393224 | tf_op jit(solution)/shard_map/ppermute | solution.py:44
  127.7 2.7 %shard_map.46.acc0_ref = f32[7,8,32,128]{3,2,1,0:T(8,128)S(1)} custom-call(f32[16,288,128]{2,1,0:T(8,128)S(1)} %all_to_all.10.blocks_ref), custom_call_target="tpu_custom_call" | custom-call | tf_op jit(solution)/shard_map/pallas_call | solution.py:384
  130.4 0.1 collective-permute-start.6
  130.5 2.7 %shard_map.47.acc1_ref = f32[7,8,32,128]{3,2,1,0:T(8,128)S(1)} custom-call(f32[16,288,128]{2,1,0:T(8,128)S(1)} %all_to_all.10.blocks_ref), custom_call_target="tpu_custom_call" | custom-call | tf_op jit(solution)/shard_map/pallas_call | solution.py:384
  133.2 0.0 collective-permute-done.4.edge_ref
  133.2 2.8 %shard_map.48.turn0_ref = f32[7,256,128]{2,1,0:T(8,128)S(1)} custom-call(f32[16,288,128]{2,1,0:T(8,128)S(1)} %all_to_all.10.blocks_ref, f32[8,16,2,128]{3,2,1,0:T(2,128)S(1)} %collective-permute-done.4.edge_ref), custom_call_target="tpu_custom_call" | custom-call | tf_op jit(solution)/shard_map/pallas_call | solution.py:459
  136.0 3.9 %collective-permute-start.7 = (f32[520,128]{1,0:T(8,128)S(1)}, f32[520,128]{1,0:T(8,128)S(1)}, u32[]{:S(2)}, u32[]{:S(2)}) collective-permute-start(f32[520,128]{1,0:T(8,128)S(1)} %get-tuple-element.30), channel_id=1, source_target_pairs={{0,15},{1,0},{2,1},{3,2},{4,3},{5,4},{6,5},{7,6},{8,7},{9,8},{10,9... | collective-permute-start | bytes 798728 | tf_op jit(solution)/shard_map/ppermute | solution.py:44
  139.9 2.3 %collective-permute-start.5 = (f32[8,16,2,128]{3,2,1,0:T(2,128)S(1)}, f32[8,16,2,128]{3,2,1,0:T(2,128)S(1)}, u32[]{:S(2)}, u32[]{:S(2)}) collective-permute-start(f32[8,16,2,128]{3,2,1,0:T(2,128)S(1)} %get-tuple-element.28), channel_id=1, source_target_pairs={{0,240},{16,0},{32,16},{48,32},{64,48},{80,64},{96,80},{112,96},{1... | collective-permute-start | bytes 393224 | tf_op jit(solution)/shard_map/ppermute | solution.py:44
  142.2 5.6 %collective-permute-done.5.edge_ref = f32[8,16,2,128]{3,2,1,0:T(2,128)S(1)} collective-permute-done((f32[8,16,2,128]{3,2,1,0:T(2,128)S(1)}, f32[8,16,2,128]{3,2,1,0:T(2,128)S(1)}, u32[]{:S(2)}, u32[]{:S(2)}) %collective-permute-start.5) | collective-permute-done | bytes 131104 | tf_op jit(solution)/shard_map/ppermute | solution.py:44
  147.9 2.8 %shard_map.49.turn1_ref = f32[7,256,128]{2,1,0:T(8,128)S(1)} custom-call(f32[16,288,128]{2,1,0:T(8,128)S(1)} %all_to_all.10.blocks_ref, f32[8,16,2,128]{3,2,1,0:T(2,128)S(1)} %collective-permute-done.5.edge_ref), custom_call_target="tpu_custom_call" | custom-call | tf_op jit(solution)/shard_map/pallas_call | solution.py:459
  150.7 0.0 collective-permute-done.6.below_ref
  150.7 0.0 collective-permute-done.7.above_ref
  150.7 6.7 %finish.1 = f32[8,16,32,128]{3,2,1,0:T(8,128)} custom-call(s32[2]{0:T(128)S(1)} %pad_add_fusion.pos_ref, f32[16,288,128]{2,1,0:T(8,128)S(1)} %all_to_all.10.blocks_ref, f32[7,8,32,128]{3,2,1,0:T(8,128)S(1)} %shard_map.46.acc0_ref, f32[7,8,32,128]{3,2,1,0:T(8,128)S(1)} %shard_map.47.acc1_ref, f32[7,256,128]{2,1,0:T(8,128)S(1)} %shard_map.48.turn0_ref, ...), custom_call_target="tpu_custom_call" | custom-call | tf_op jit(solution)/shard_map/finish/pallas_call | solution.py:518
  (2 shorter events, 0.0 us)
Async XLA Ops:
  3.4 59.2 %all-to-all-start = ((f32[16,8,32,128]{3,2,1,0:T(8,128)}), f32[16,8,32,128]{3,2,1,0:T(8,128)S(1)}, u32[]{:S(2)}, u32[]{:S(2)}) async-start(f32[16,8,32,128]{3,2,1,0:T(8,128)} %pack.1), calls=%async_computation | async-start | bytes 4194304 | tf_op jit(solution)/shard_map/all_to_all | solution.py:536
  14.5 21.9 %copy-start.1 = (s32[16]{0:T(128)S(1)}, s32[16]{0:T(128)}, u32[]{:S(2)}) copy-start(s32[16]{0:T(128)} %constant.41.clone..sunk.2) | copy-start | bytes 196
  14.5 48.1 %copy-start = (s32[256]{0:T(256)S(1)}, s32[256]{0:T(256)}, u32[]{:S(2)}) copy-start(s32[256]{0:T(256)} %offsets_ref.1) | copy-start | bytes 3076
  18.1 5.3 %collective-permute-start = (f32[8,128]{1,0:T(8,128)S(1)}, f32[8,128]{1,0:T(8,128)S(1)}, u32[]{:S(2)}, u32[]{:S(2)}) collective-permute-start(f32[8,128]{1,0:T(8,128)S(1)} %broadcast_in_dim.8), channel_id=1, source_target_pairs={{0,1},{1,2},{2,3},{3,4},{4,5},{5,6},{6,7},{7,8},{8,9},{9,10},{10,1... | collective-permute-start | bytes 12296 | tf_op jit(solution)/shard_map/ppermute | solution.py:44
  24.1 11.6 %collective-permute-start.1 = (f32[8,128]{1,0:T(8,128)S(1)}, f32[8,128]{1,0:T(8,128)S(1)}, u32[]{:S(2)}, u32[]{:S(2)}) collective-permute-start(f32[8,128]{1,0:T(8,128)S(1)} %broadcast_maximum_fusion), channel_id=1, source_target_pairs={{0,2},{1,3},{2,4},{3,5},{4,6},{5,7},{6,8},{7,9},{8,10},{9,11},{10,... | collective-permute-start | bytes 12296 | tf_op jit(solution)/shard_map/ppermute | solution.py:44
  36.3 4.9 %collective-permute-start.2 = (f32[8,128]{1,0:T(8,128)S(1)}, f32[8,128]{1,0:T(8,128)S(1)}, u32[]{:S(2)}, u32[]{:S(2)}) collective-permute-start(f32[8,128]{1,0:T(8,128)S(1)} %fusion.25), channel_id=1, source_target_pairs={{0,4},{1,5},{2,6},{3,7},{4,8},{5,9},{6,10},{7,11},{8,12},{9,13},{1... | collective-permute-start | bytes 12296 | tf_op jit(solution)/shard_map/ppermute | solution.py:44
  41.2 5.1 %collective-permute-start.3 = (f32[8,128]{1,0:T(8,128)S(1)}, f32[8,128]{1,0:T(8,128)S(1)}, u32[]{:S(2)}, u32[]{:S(2)}) collective-permute-start(f32[8,128]{1,0:T(8,128)S(1)} %max.26), channel_id=1, source_target_pairs={{0,8},{1,9},{2,10},{3,11},{4,12},{5,13},{6,14},{7,15},{8,0},{9,1},... | collective-permute-start | bytes 12296 | tf_op jit(solution)/shard_map/ppermute | solution.py:44
  125.5 7.7 %collective-permute-start.4 = (f32[8,16,2,128]{3,2,1,0:T(2,128)S(1)}, f32[8,16,2,128]{3,2,1,0:T(2,128)S(1)}, u32[]{:S(2)}, u32[]{:S(2)}) collective-permute-start(f32[8,16,2,128]{3,2,1,0:T(2,128)S(1)} %get-tuple-element.22), channel_id=1, source_target_pairs={{0,16},{16,32},{32,48},{48,64},{64,80},{80,96},{96,112},{112,128},... | collective-permute-start | bytes 393224 | tf_op jit(solution)/shard_map/ppermute | solution.py:44
  130.4 20.3 %collective-permute-start.6 = (f32[520,128]{1,0:T(8,128)S(1)}, f32[520,128]{1,0:T(8,128)S(1)}, u32[]{:S(2)}, u32[]{:S(2)}) collective-permute-start(f32[520,128]{1,0:T(8,128)S(1)} %get-tuple-element.29), channel_id=1, source_target_pairs={{0,1},{1,2},{2,3},{3,4},{4,5},{5,6},{6,7},{7,8},{8,9},{9,10},{10,1... | collective-permute-start | bytes 798728 | tf_op jit(solution)/shard_map/ppermute | solution.py:44
  136.0 14.7 %collective-permute-start.7 = (f32[520,128]{1,0:T(8,128)S(1)}, f32[520,128]{1,0:T(8,128)S(1)}, u32[]{:S(2)}, u32[]{:S(2)}) collective-permute-start(f32[520,128]{1,0:T(8,128)S(1)} %get-tuple-element.30), channel_id=1, source_target_pairs={{0,15},{1,0},{2,1},{3,2},{4,3},{5,4},{6,5},{7,6},{8,7},{9,8},{10,9... | collective-permute-start | bytes 798728 | tf_op jit(solution)/shard_map/ppermute | solution.py:44
  139.9 7.9 %collective-permute-start.5 = (f32[8,16,2,128]{3,2,1,0:T(2,128)S(1)}, f32[8,16,2,128]{3,2,1,0:T(2,128)S(1)}, u32[]{:S(2)}, u32[]{:S(2)}) collective-permute-start(f32[8,16,2,128]{3,2,1,0:T(2,128)S(1)} %get-tuple-element.28), channel_id=1, source_target_pairs={{0,240},{16,0},{32,16},{48,32},{64,48},{80,64},{96,80},{112,96},{1... | collective-permute-start | bytes 393224 | tf_op jit(solution)/shard_map/ppermute | solution.py:44

commit v3 on v2

--- a/solution.py
+++ b/solution.py
@@ -282,26 +282,32 @@
     ghost = jax.ShapeDtypeStruct((GHOSTS + 8, DEPTH), jnp.float32)
     edge = jax.ShapeDtypeStruct((FIELDS, ROWS, 2, DEPTH), jnp.float32)
 
-    def kernel(pos_ref, blocks_ref, left_ref, right_ref, up_ref, down_ref):
+    def kernel(pos_ref, blocks_ref, az0_ref, az1_ref, rad0_ref, rad1_ref):
         group = pos_ref[1]
-        top_at = pl.multiple_of(jnp.where(group == GROUPS - 1, EXTRA, CELLS), 8)
-        low_at = pl.multiple_of(jnp.where(group == 0, EXTRA, 0), 8)
+        rad_even = (group & 1) == 0
+        az_even = pos_ref[2] == 0
+        top_at = jnp.where(group == GROUPS - 1, EXTRA, CELLS)
+        low_at = jnp.where(group == 0, EXTRA, 0)
         for f in range(FIELDS):
             for u, pair in enumerate(PAIRS):
                 for r in range(2):
                     h = (2 * pair + r + 2 * f) % HOLDERS
-                    right_ref[f, 2 * pair + r] = blocks_ref[
-                        h, (u + 1) * CELLS - 2:(u + 1) * CELLS, :]
-                    left_ref[f, 2 * pair + r] = blocks_ref[h, u * CELLS:u * CELLS + 2, :]
+                    right = blocks_ref[h, (u + 1) * CELLS - 2:(u + 1) * CELLS, :]
+                    left = blocks_ref[h, u * CELLS:u * CELLS + 2, :]
+                    az0_ref[f, 2 * pair + r] = jnp.where(az_even, right, left)
+                    az1_ref[f, 2 * pair + r] = jnp.where(az_even, left, right)
             for r in range(2):
                 top = (ROWS - 2 + r + 2 * f) % HOLDERS
                 low = (r + 2 * f) % HOLDERS
                 at = (2 * f + r) * CELLS
-                up_ref[at:at + CELLS, :] = blocks_ref[top, pl.ds(top_at, CELLS), :]
-                down_ref[at:at + CELLS, :] = blocks_ref[low, pl.ds(low_at, CELLS), :]
+                for even, ref in ((True, rad0_ref), (False, rad1_ref)):
+                    up = rad_even if even else jnp.logical_not(rad_even)
+                    h = jnp.where(up, top, low)
+                    start = pl.multiple_of(jnp.where(up, top_at, low_at), 8)
+                    ref[at:at + CELLS, :] = blocks_ref[h, pl.ds(start, CELLS), :]
         peak = peak_of(blocks_ref)
-        up_ref[GHOSTS:, :] = peak
-        down_ref[GHOSTS:, :] = peak
+        rad0_ref[GHOSTS:, :] = peak
+        rad1_ref[GHOSTS:, :] = peak
 
     return pl.pallas_call(
         kernel,
@@ -329,13 +335,14 @@
             for f in range(FIELDS)]
 
 
-def vertical(blocks, first, rows):
+def vertical(blocks):
     order = order_of(3)
     slots = flux_slots(3)
+    rows = ROWS
 
     def kernel(blocks_ref, acc_ref, left_ref, right_ref, flux_ref):
         def states(r):
-            prim = to_primitive(load(blocks_ref, first + r, 0, CELLS))
+            prim = to_primitive(load(blocks_ref, r, 0, CELLS))
             for k, f in enumerate(order):
                 value = prim[f]
                 below = pltpu.roll(value, 1, 1)
@@ -351,7 +358,7 @@
                 flux_ref[k, r] = flux[k]
 
         def changes(r):
-            state = load(blocks_ref, first + r, 0, CELLS)
+            state = load(blocks_ref, r, 0, CELLS)
             gains = [
                 None,
                 2.0 * OMEGA * state[2],
@@ -387,7 +394,8 @@
         in_specs=[VMEM],
         out_specs=VMEM,
         scratch_shapes=[sides, sides, sides],
-        compiler_params=params(16),
+        compiler_params=params(20),
+        name="vertical",
     )(blocks)
 
 
@@ -430,50 +438,56 @@
     lax.fori_loop(0, ROWS, body, 0)
 
 
-def azimuthal(blocks, edge, half):
-    first = half * (CELLS // 2)
-
-    def kernel(blocks_ref, edge_ref, turn_ref, prim_ref):
-        fill(blocks_ref, prim_ref, 0, 8 * half, CELLS - 8)
-        at = PAD + CELLS if half else PAD - 2
+def azimuthal(pos, blocks, edge0, edge1):
+    def kernel(pos_ref, blocks_ref, edge0_ref, edge1_ref, turn_ref, prim_ref):
+        even = pos_ref[2] == 0
+        fill(blocks_ref, prim_ref, 0, 0, CELLS)
 
         def sides(i, carry):
-            values = to_primitive([edge_ref[f, i] for f in range(FIELDS)])
-            for f in range(FIELDS):
-                prim_ref[f, pl.ds(pl.multiple_of(i * WIDE, 8) + at, 2), :] = values[f]
+            base = pl.multiple_of(i * WIDE, 8)
+            first = [edge0_ref[f, i] for f in range(FIELDS)]
+            second = [edge1_ref[f, i] for f in range(FIELDS)]
+            for at, a, b in ((PAD - 2, second, first), (PAD + CELLS, first, second)):
+                values = to_primitive([jnp.where(even, x, y) for x, y in zip(a, b)])
+                for f in range(FIELDS):
+                    prim_ref[f, pl.ds(base + at, 2), :] = values[f]
             return carry
 
         lax.fori_loop(0, ROWS, sides, 0, unroll=4)
 
         def rows_at(a):
             return [jnp.concatenate([
-                prim_ref[f, pl.ds(g * WIDE + PAD + first + a, 8, stride=WIDE), :]
+                prim_ref[f, pl.ds(g * WIDE + PAD + a, 8, stride=WIDE), :]
                 for g in range(0, ROWS, 8)], axis=0) for f in range(FIELDS)]
 
         def keep(a, lower, upper):
             for k in range(7):
                 turn_ref[k, pl.ds(pl.multiple_of(a * ROWS, 8), ROWS), :] = lower[k] - upper[k]
 
-        march(order_of(2), rows_at, [(0, CELLS // 2, keep)])
+        march(order_of(2), rows_at, [(0, CELLS, keep)])
 
     return pl.pallas_call(
         kernel,
-        out_shape=jax.ShapeDtypeStruct((7, CELLS // 2 * ROWS, DEPTH), jnp.float32),
-        in_specs=[VMEM] * 2,
+        out_shape=jax.ShapeDtypeStruct((7, CELLS * ROWS, DEPTH), jnp.float32),
+        in_specs=[SMEM] + [VMEM] * 3,
         out_specs=VMEM,
         scratch_shapes=[pltpu.VMEM((FIELDS, ROWS * WIDE, DEPTH), jnp.float32)],
         compiler_params=params(12),
-    )(blocks, edge)
-
-
-def finish(pos, blocks, accs, turns, below, above):
-    def kernel(pos_ref, blocks_ref, acc0_ref, acc1_ref, turn0_ref, turn1_ref, below_ref, above_ref,
+        name="azimuthal",
+    )(pos, blocks, edge0, edge1)
+
+
+def finish(pos, blocks, acc, turn, ghost0, ghost1):
+    def kernel(pos_ref, blocks_ref, acc_ref, turn_ref, ghost0_ref, ghost1_ref,
                out_ref, prim_ref):
+        group = pos_ref[1]
+        even = (group & 1) == 0
         fill(blocks_ref, prim_ref, 2, 0, CELLS)
-        for ghost_ref, row in ((below_ref, 0), (above_ref, ROWS + 2)):
+        for a_ref, b_ref, row in ((ghost1_ref, ghost0_ref, 0), (ghost0_ref, ghost1_ref, ROWS + 2)):
             for r in range(2):
                 values = to_primitive([
-                    ghost_ref[(2 * f + r) * CELLS:(2 * f + r + 1) * CELLS, :]
+                    jnp.where(even, a_ref[(2 * f + r) * CELLS:(2 * f + r + 1) * CELLS, :],
+                              b_ref[(2 * f + r) * CELLS:(2 * f + r + 1) * CELLS, :])
                     for f in range(FIELDS)])
                 at = (row + r) * WIDE + PAD
                 for f in range(FIELDS):
@@ -481,49 +495,44 @@
 
         a_slots = flux_slots(2)
         slots = flux_slots(1)
-        group = pos_ref[1]
-        peak = jnp.where(
-            group == 0, above_ref[GHOSTS:, :],
-            jnp.where(group == GROUPS - 1, below_ref[GHOSTS:, :], peak_of(blocks_ref)))
+        peak = jnp.where((group == 0) | (group == GROUPS - 1),
+                         ghost0_ref[GHOSTS:, :], peak_of(blocks_ref))
         dt = CFL_NUMBER / peak[0:1]
 
-        for start, turn_ref in ((0, turn0_ref), (R_BLOCK, turn1_ref)):
+        for start in (0, R_BLOCK):
             part = slice(start, start + R_BLOCK)
 
             def cells_at(i):
                 at = pl.multiple_of((i + 2) * WIDE, 8) + PAD + start
                 return [prim_ref[f, pl.ds(at, R_BLOCK), :] for f in range(FIELDS)]
 
-            def update(acc_ref, first, i, lower, upper):
+            def update(i, lower, upper):
                 state = load(blocks_ref, i, start, R_BLOCK)
                 change = [None] * FIELDS
                 for k, slot in enumerate(slots):
                     change[slot] = lower[k] - upper[k]
                 for k, slot in enumerate(a_slots):
                     turn = jnp.concatenate([
-                        turn_ref[k, pl.ds(g * ROWS + i, 8, stride=ROWS), :]
+                        turn_ref[k, pl.ds((start + g) * ROWS + i, 8, stride=ROWS), :]
                         for g in range(0, R_BLOCK, 8)], axis=0)
                     change[slot] = turn if change[slot] is None else change[slot] + turn
                 for slot in range(FIELDS - 1):
-                    total = acc_ref[slot, i - first, part, :]
+                    total = acc_ref[slot, i, part, :]
                     total = total if change[slot] is None else total + change[slot]
                     out_ref[slot, i, part, :] = state[slot] + dt * total
                 out_ref[7, i, part, :] = state[7] + dt * change[7]
 
-            half = ROWS // 2
-            march(order_of(1), cells_at, [
-                (0, half, functools.partial(update, acc0_ref, 0)),
-                (half, ROWS, functools.partial(update, acc1_ref, half))])
+            march(order_of(1), cells_at, [(0, ROWS, update)])
 
     return pl.pallas_call(
         kernel,
         out_shape=jax.ShapeDtypeStruct((FIELDS, ROWS, CELLS, DEPTH), jnp.float32),
-        in_specs=[SMEM] + [VMEM] * 7,
+        in_specs=[SMEM] + [VMEM] * 5,
         out_specs=VMEM,
         scratch_shapes=[pltpu.VMEM((FIELDS, (ROWS + 4) * WIDE, DEPTH), jnp.float32)],
         compiler_params=params(20),
         name="finish",
-    )(pos, blocks, *accs, *turns, below, above)
+    )(pos, blocks, acc, turn, ghost0, ghost1)
 
 
 def over(peak, axis):
@@ -539,24 +548,26 @@
 
 def local(fields, offsets, boundary_shift):
     holder = jnp.take(jnp.array(HOLDER, jnp.int32), lax.axis_index(AZ))
-    pos = jnp.stack([holder, lax.axis_index(RAD).astype(jnp.int32)])
+    az = lax.axis_index(AZ).astype(jnp.int32)
+    pos = jnp.stack([holder, lax.axis_index(RAD).astype(jnp.int32), az & 1])
     rings = exchanged(pack(fields), ORDER)
     peak = jnp.broadcast_to(jnp.max(cell_speed(to_primitive(fields))), (8, DEPTH))
     peak = over(peak, RAD)
     blocks = exchanged(rotate_rings(pos, offsets, boundary_shift, rings, peak), BACK)
-    left, right, up, down = rims(pos, blocks)
-    before = passed_along(right, AZ, 1)
-    acc0 = vertical(blocks, 0, ROWS // 2)
-    acc0, up, blocks = lax.optimization_barrier((acc0, up, blocks))
-    below = passed_along(up, RAD, 1)
-    acc1 = vertical(blocks, ROWS // 2, ROWS // 2)
-    acc1, left, blocks = lax.optimization_barrier((acc1, left, blocks))
-    after = passed_along(left, AZ, -1)
-    turn0 = azimuthal(blocks, before, 0)
-    turn0, down, blocks = lax.optimization_barrier((turn0, down, blocks))
-    above = passed_along(down, RAD, -1)
-    turn1 = azimuthal(blocks, after, 1)
-    return finish(pos, blocks, (acc0, acc1), (turn0, turn1), below, above)
+    az0, az1, rad0, rad1 = rims(pos, blocks)
+    edge0 = swapped(az0, AZ, 0)
+    edge1 = swapped(az1, AZ, 1)
+    ghost0 = swapped(rad0, RAD, 0)
+    ghost1 = swapped(rad1, RAD, 1)
+    acc = vertical(blocks)
+    turn = azimuthal(pos, blocks, edge0, edge1)
+    return finish(pos, blocks, acc, turn, ghost0, ghost1)
+
+
+def swapped(array, axis, odd):
+    devices = lax.axis_size(axis)
+    return lax.ppermute(array, axis, [
+        (i, (i + (1 if (i + odd) % 2 == 0 else -1)) % devices) for i in range(devices)])
 
 
 def solution(mesh):

time: 158 us -> 155 us (0.981)
  the two profiles are of different devices: /device:TPU:32 before, /device:TPU:24 now
where the time goes in v3:
time: 155 us
  blocking collectives  58.8 us (38%)
  waiting for transfers between devices  43.1 us (28%)
  Pallas kernels  23.1 us (15%)
  starting transfers between devices  22.8 us (15%)
  other arithmetic  4.33 us (3%)
    all_to_all x1, blocking collectives, exchanged(): lax.all_to_all(units, AZ, split_axis=0, concat_axis=0, tiled=True, axis_i...  58.8 us
    all_to_all x1, waiting for transfers between devices, exchanged(): lax.all_to_all(units, AZ, split_axis=0, concat_axis=0, tiled=True, axis_i...  27.9 us
    all_to_all x1, starting transfers between devices, exchanged(): lax.all_to_all(units, AZ, split_axis=0, concat_axis=0, tiled=True, axis_i...  11 us
    ppermute x4, waiting for transfers between devices, passed_along(): lax.ppermute(array, axis, [(i, (i + by) % devices) for i in range(devices)])  10.8 us
    pallas_call x1, Pallas kernels, finish(): pl.pallas_call(kernel, out_shape=jax.ShapeDtypeStruct((FIELDS, ROWS, CELL...  6.79 us
    ppermute x4, starting transfers between devices, swapped(): lax.ppermute(array, axis, [(i, (i + (1 if (i + odd) % 2 == 0 else -1)) %...  6.61 us
    pallas_call x1, Pallas kernels, azimuthal(): pl.pallas_call(kernel, out_shape=jax.ShapeDtypeStruct((7, CELLS * ROWS, D...  5.64 us
    pallas_call x1, Pallas kernels, vertical(): pl.pallas_call(kernel, out_shape=jax.ShapeDtypeStruct((FIELDS - 1, rows,...  5.29 us
  transfers between devices with their start and end apart: 9, of which 6 were waited for; matrix products, arithmetic and copies ran while one was open for 4% of the time, Pallas kernels for 7%

profile of v3, /device:TPU:24, one launch (start us, length us, event | category | flops | bytes accessed | tf_op | source)
XLA Modules:
  0.0 154.7 jit_solution(13940692259840288495)
XLA Ops:
  0.0 3.4 %pack.1 = f32[16,8,32,128]{3,2,1,0:T(8,128)} custom-call(f32[8,16,32,128]{3,2,1,0:T(8,128)} %fields_ref.1), custom_call_target="tpu_custom_call" | custom-call | tf_op jit(solution)/shard_map/pack/pallas_call | solution.py:215
  3.4 11.0 %all-to-all-start = ((f32[16,8,32,128]{3,2,1,0:T(8,128)}), f32[16,8,32,128]{3,2,1,0:T(8,128)S(1)}, u32[]{:S(2)}, u32[]{:S(2)}) async-start(f32[16,8,32,128]{3,2,1,0:T(8,128)} %pack.1), calls=%async_computation | async-start | bytes 4194304 | tf_op jit(solution)/shard_map/all_to_all | solution.py:545
  14.5 0.0 copy-start.1
  14.5 0.0 copy-start
  14.5 3.0 %add_reduce_fusion = f32[]{:T(128)} fusion(f32[8,16,32,128]{3,2,1,0:T(8,128)} %fields_ref.1), kind=kLoop, calls=%fused_computation.40 | loop fusion | flops 3538943 | bytes 2097156 | tf_op jit(solution)/shard_map/reduce_max | solution.py:554
  17.5 0.6 broadcast_in_dim.8
  18.1 0.1 collective-permute-start
  18.2 4.0 %collective-permute-done = f32[8,128]{1,0:T(8,128)S(1)} collective-permute-done((f32[8,128]{1,0:T(8,128)S(1)}, f32[8,128]{1,0:T(8,128)S(1)}, u32[]{:S(2)}, u32[]{:S(2)}) %collective-permute-start) | collective-permute-done | bytes 4128 | tf_op jit(solution)/shard_map/ppermute | solution.py:44
  22.2 0.6 broadcast_maximum_fusion
  22.8 0.3 collective-permute-start.1
  23.2 4.3 %collective-permute-done.1 = f32[8,128]{1,0:T(8,128)S(1)} collective-permute-done((f32[8,128]{1,0:T(8,128)S(1)}, f32[8,128]{1,0:T(8,128)S(1)}, u32[]{:S(2)}, u32[]{:S(2)}) %collective-permute-start.1) | collective-permute-done | bytes 4128 | tf_op jit(solution)/shard_map/ppermute | solution.py:44
  27.4 0.6 fusion.25
  28.1 2.8 %collective-permute-start.2 = (f32[8,128]{1,0:T(8,128)S(1)}, f32[8,128]{1,0:T(8,128)S(1)}, u32[]{:S(2)}, u32[]{:S(2)}) collective-permute-start(f32[8,128]{1,0:T(8,128)S(1)} %fusion.25), channel_id=1, source_target_pairs={{0,4},{1,5},{2,6},{3,7},{4,8},{5,9},{6,10},{7,11},{8,12},{9,13},{1... | collective-permute-start | bytes 12296 | tf_op jit(solution)/shard_map/ppermute | solution.py:44
  30.9 0.0 copy-done.1
  30.9 0.6 dynamic-slice.4
  32.0 0.2 collective-permute-done.2
  32.2 1.9 %collective-permute-start.3 = (f32[8,128]{1,0:T(8,128)S(1)}, f32[8,128]{1,0:T(8,128)S(1)}, u32[]{:S(2)}, u32[]{:S(2)}) collective-permute-start(f32[8,128]{1,0:T(8,128)S(1)} %max.26), channel_id=1, source_target_pairs={{0,8},{1,9},{2,10},{3,11},{4,12},{5,13},{6,14},{7,15},{8,0},{9,1},... | collective-permute-start | bytes 12296 | tf_op jit(solution)/shard_map/ppermute | solution.py:44
  34.2 0.1 pad_add_fusion.pos_ref
  34.9 2.4 %collective-permute-done.3 = f32[8,128]{1,0:T(8,128)S(1)} collective-permute-done((f32[8,128]{1,0:T(8,128)S(1)}, f32[8,128]{1,0:T(8,128)S(1)}, u32[]{:S(2)}, u32[]{:S(2)}) %collective-permute-start.3) | collective-permute-done | bytes 4128 | tf_op jit(solution)/shard_map/ppermute | solution.py:44
  37.3 27.9 %all-to-all-done.ring_ref = f32[16,8,32,128]{3,2,1,0:T(8,128)S(1)} async-done(((f32[16,8,32,128]{3,2,1,0:T(8,128)}), f32[16,8,32,128]{3,2,1,0:T(8,128)S(1)}, u32[]{:S(2)}, u32[]{:S(2)}) %all-to-all-start) | async-done | bytes 2097184 | tf_op jit(solution)/shard_map/all_to_all | solution.py:545
  65.2 0.0 copy-done
  65.2 1.2 rotate.1
  66.5 58.8 %all_to_all.10.blocks_ref = f32[16,288,128]{2,1,0:T(8,128)S(1)} all-to-all(f32[16,288,128]{2,1,0:T(8,128)S(1)} %rotate.1), channel_id=1, replica_groups={{144,112,176,80,208,48,240,16,128,96,160,64,192,32,224,0},{145,113,177,..., dimensions={0} | all-to-all | bytes 4718592 | tf_op jit(solution)/shard_map/all_to_all | solution.py:545
  125.2 0.7 rims.1
  125.9 0.1 collective-permute-start.6
  126.0 0.9 collective-permute-start.7
  126.9 3.2 %collective-permute-start.4 = (f32[8,16,2,128]{3,2,1,0:T(2,128)S(1)}, f32[8,16,2,128]{3,2,1,0:T(2,128)S(1)}, u32[]{:S(2)}, u32[]{:S(2)}) collective-permute-start(f32[8,16,2,128]{3,2,1,0:T(2,128)S(1)} %get-tuple-element.9), channel_id=1, source_target_pairs={{0,16},{16,0},{32,48},{48,32},{64,80},{80,64},{96,112},{112,96},{1... | collective-permute-start | bytes 393224 | tf_op jit(solution)/shard_map/ppermute | solution.py:569
  130.1 2.4 %collective-permute-start.5 = (f32[8,16,2,128]{3,2,1,0:T(2,128)S(1)}, f32[8,16,2,128]{3,2,1,0:T(2,128)S(1)}, u32[]{:S(2)}, u32[]{:S(2)}) collective-permute-start(f32[8,16,2,128]{3,2,1,0:T(2,128)S(1)} %get-tuple-element.10), channel_id=1, source_target_pairs={{0,240},{16,32},{32,16},{48,64},{64,48},{80,96},{96,80},{112,128},... | collective-permute-start | bytes 393224 | tf_op jit(solution)/shard_map/ppermute | solution.py:569
  132.5 5.3 %vertical.1.acc_ref = f32[7,16,32,128]{3,2,1,0:T(8,128)S(1)} custom-call(f32[16,288,128]{2,1,0:T(8,128)S(1)} %all_to_all.10.blocks_ref), custom_call_target="tpu_custom_call" | custom-call | tf_op jit(solution)/shard_map/vertical/pallas_call | solution.py:391
  137.8 4.4 %collective-permute-done.4.edge0_ref = f32[8,16,2,128]{3,2,1,0:T(2,128)S(1)} collective-permute-done((f32[8,16,2,128]{3,2,1,0:T(2,128)S(1)}, f32[8,16,2,128]{3,2,1,0:T(2,128)S(1)}, u32[]{:S(2)}, u32[]{:S(2)}) %collective-permute-start.4) | collective-permute-done | bytes 131104 | tf_op jit(solution)/shard_map/ppermute | solution.py:569
  142.2 0.0 collective-permute-done.5.edge1_ref
  142.2 5.6 %azimuthal.1.turn_ref = f32[7,512,128]{2,1,0:T(8,128)S(1)} custom-call(s32[3]{0:T(128)S(1)} %pad_add_fusion.pos_ref, f32[16,288,128]{2,1,0:T(8,128)S(1)} %all_to_all.10.blocks_ref, f32[8,16,2,128]{3,2,1,0:T(2,128)S(1)} %collective-permute-done.4.edge0_ref, f32[8,16,2,128]{3,2,1,0:T(2,128)S(1)} %collective-permute-done.5.edge1_ref), custom_call_target="tpu_custom_call" | custom-call | tf_op jit(solution)/shard_map/azimuthal/pallas_call | solution.py:469
  147.9 0.0 collective-permute-done.6.ghost0_ref
  147.9 0.0 collective-permute-done.7.ghost1_ref
  147.9 6.8 %finish.1 = f32[8,16,32,128]{3,2,1,0:T(8,128)} custom-call(s32[3]{0:T(128)S(1)} %pad_add_fusion.pos_ref, f32[16,288,128]{2,1,0:T(8,128)S(1)} %all_to_all.10.blocks_ref, f32[7,16,32,128]{3,2,1,0:T(8,128)S(1)} %vertical.1.acc_ref, f32[7,512,128]{2,1,0:T(8,128)S(1)} %azimuthal.1.turn_ref, f32[520,128]{1,0:T(8,128)S(1)} %collective-permute-done.6.ghost0_ref, ...), custom_call_target="tpu_custom_call" | custom-call | tf_op jit(solution)/shard_map/finish/pallas_call | solution.py:527
  (2 shorter events, 0.0 us)
Async XLA Ops:
  3.4 61.8 %all-to-all-start = ((f32[16,8,32,128]{3,2,1,0:T(8,128)}), f32[16,8,32,128]{3,2,1,0:T(8,128)S(1)}, u32[]{:S(2)}, u32[]{:S(2)}) async-start(f32[16,8,32,128]{3,2,1,0:T(8,128)} %pack.1), calls=%async_computation | async-start | bytes 4194304 | tf_op jit(solution)/shard_map/all_to_all | solution.py:545
  14.5 16.4 %copy-start.1 = (s32[16]{0:T(128)S(1)}, s32[16]{0:T(128)}, u32[]{:S(2)}) copy-start(s32[16]{0:T(128)} %constant.43.clone..sunk.2) | copy-start | bytes 196
  14.5 50.7 %copy-start = (s32[256]{0:T(256)S(1)}, s32[256]{0:T(256)}, u32[]{:S(2)}) copy-start(s32[256]{0:T(256)} %offsets_ref.1) | copy-start | bytes 3076
  18.1 4.1 %collective-permute-start = (f32[8,128]{1,0:T(8,128)S(1)}, f32[8,128]{1,0:T(8,128)S(1)}, u32[]{:S(2)}, u32[]{:S(2)}) collective-permute-start(f32[8,128]{1,0:T(8,128)S(1)} %broadcast_in_dim.8), channel_id=1, source_target_pairs={{0,1},{1,2},{2,3},{3,4},{4,5},{5,6},{6,7},{7,8},{8,9},{9,10},{10,1... | collective-permute-start | bytes 12296 | tf_op jit(solution)/shard_map/ppermute | solution.py:44
  22.8 4.6 %collective-permute-start.1 = (f32[8,128]{1,0:T(8,128)S(1)}, f32[8,128]{1,0:T(8,128)S(1)}, u32[]{:S(2)}, u32[]{:S(2)}) collective-permute-start(f32[8,128]{1,0:T(8,128)S(1)} %broadcast_maximum_fusion), channel_id=1, source_target_pairs={{0,2},{1,3},{2,4},{3,5},{4,6},{5,7},{6,8},{7,9},{8,10},{9,11},{10,... | collective-permute-start | bytes 12296 | tf_op jit(solution)/shard_map/ppermute | solution.py:44
  28.1 4.1 %collective-permute-start.2 = (f32[8,128]{1,0:T(8,128)S(1)}, f32[8,128]{1,0:T(8,128)S(1)}, u32[]{:S(2)}, u32[]{:S(2)}) collective-permute-start(f32[8,128]{1,0:T(8,128)S(1)} %fusion.25), channel_id=1, source_target_pairs={{0,4},{1,5},{2,6},{3,7},{4,8},{5,9},{6,10},{7,11},{8,12},{9,13},{1... | collective-permute-start | bytes 12296 | tf_op jit(solution)/shard_map/ppermute | solution.py:44
  32.2 5.1 %collective-permute-start.3 = (f32[8,128]{1,0:T(8,128)S(1)}, f32[8,128]{1,0:T(8,128)S(1)}, u32[]{:S(2)}, u32[]{:S(2)}) collective-permute-start(f32[8,128]{1,0:T(8,128)S(1)} %max.26), channel_id=1, source_target_pairs={{0,8},{1,9},{2,10},{3,11},{4,12},{5,13},{6,14},{7,15},{8,0},{9,1},... | collective-permute-start | bytes 12296 | tf_op jit(solution)/shard_map/ppermute | solution.py:44
  125.9 21.9 %collective-permute-start.6 = (f32[520,128]{1,0:T(8,128)S(1)}, f32[520,128]{1,0:T(8,128)S(1)}, u32[]{:S(2)}, u32[]{:S(2)}) collective-permute-start(f32[520,128]{1,0:T(8,128)S(1)} %get-tuple-element.11), channel_id=1, source_target_pairs={{0,1},{1,0},{2,3},{3,2},{4,5},{5,4},{6,7},{7,6},{8,9},{9,8},{10,11... | collective-permute-start | bytes 798728 | tf_op jit(solution)/shard_map/ppermute | solution.py:569
  126.0 21.9 %collective-permute-start.7 = (f32[520,128]{1,0:T(8,128)S(1)}, f32[520,128]{1,0:T(8,128)S(1)}, u32[]{:S(2)}, u32[]{:S(2)}) collective-permute-start(f32[520,128]{1,0:T(8,128)S(1)} %get-tuple-element.12), channel_id=1, source_target_pairs={{0,15},{1,2},{2,1},{3,4},{4,3},{5,6},{6,5},{7,8},{8,7},{9,10},{10,... | collective-permute-start | bytes 798728 | tf_op jit(solution)/shard_map/ppermute | solution.py:569
  126.9 15.3 %collective-permute-start.4 = (f32[8,16,2,128]{3,2,1,0:T(2,128)S(1)}, f32[8,16,2,128]{3,2,1,0:T(2,128)S(1)}, u32[]{:S(2)}, u32[]{:S(2)}) collective-permute-start(f32[8,16,2,128]{3,2,1,0:T(2,128)S(1)} %get-tuple-element.9), channel_id=1, source_target_pairs={{0,16},{16,0},{32,48},{48,32},{64,80},{80,64},{96,112},{112,96},{1... | collective-permute-start | bytes 393224 | tf_op jit(solution)/shard_map/ppermute | solution.py:569
  130.1 12.1 %collective-permute-start.5 = (f32[8,16,2,128]{3,2,1,0:T(2,128)S(1)}, f32[8,16,2,128]{3,2,1,0:T(2,128)S(1)}, u32[]{:S(2)}, u32[]{:S(2)}) collective-permute-start(f32[8,16,2,128]{3,2,1,0:T(2,128)S(1)} %get-tuple-element.10), channel_id=1, source_target_pairs={{0,240},{16,32},{32,16},{48,64},{64,48},{80,96},{96,80},{112,128},... | collective-permute-start | bytes 393224 | tf_op jit(solution)/shard_map/ppermute | solution.py:569
